TPU v7x, 128 devices: a whole 4x4x4 slice. The times are simulated.
128 devices in a mesh: row: 16 (over y, x_hi, core), tensor: 8 (over x_lo, z).
Axes of the slice: x: 4 (x_hi: 2, x_lo: 2; x = x_hi * 2 + x_lo), y: 4, z: 4, core: 2. Of those that a mesh axis runs over, the one named last changes fastest.
Arguments:
- hidden_rows: bfloat16 [4096, 8192], P('row'), may hold values from -6 to 6
- w_query: bfloat16 [8192, 8192], P('row', 'tensor'), may hold values from -0.0625 to 0.0625
- w_out: bfloat16 [8192, 8192], P('tensor', 'row'), may hold values from -0.0625 to 0.0625
- pack_key_cache: bfloat16 [131072, 1024], P('row', 'tensor'), may hold values from -250 to 250
- pack_value_cache: bfloat16 [131072, 1024], P('row', 'tensor'), may hold values from -6 to 6
- query_pos: int32 [4096], P('row'), may hold values from 0 to 131071, as said below
- doc_blocks: int32 [16, 4], P('row'), may hold values from 1 to 32, 64 in all within a row
Outputs:
- mixed: bfloat16 [4096, 8192], P('row', 'tensor')
Inputs may be any that keep to these rules, and one draw needn't show every extreme that they name: `query_pos`: each index of row holds 256 consecutive query rows; at most 32 of them lie in any one block of 8192 key positions, and exactly 32 in some blocks. Positions may repeat. `doc_blocks`: each row sums to 64.
All inputs are finite; a program needn't handle non-finite values.
Results may differ from a plain program's by a relative error of at most 0.014.
The roundings to bfloat16 on the way count: a program that leaves them out, or rounds other values in their place, can miss the bound.
Values may be sent and summed in bfloat16 or wider, within the bound.
No kernel may reach another device: no remote copies, remote signals or barrier semaphores. Data moves between devices by JAX's collectives and lax.ppermute only.
A program may use at most 128 MiB of HBM per device.

v0:
```python
import functools
import math

import jax
import jax.numpy as jnp
from jax import lax
from jax.experimental import pallas as pl
from jax.experimental.pallas import tpu as pltpu
from jax.sharding import PartitionSpec as P


HEAD_SIZE = 128
NEG = -1e30
TILE = 64
KB = 1024
CHAIN = 128
N_Y, N_XH, N_CORE = 4, 2, 2
N_XL, N_Z = 2, 4
DEPTH = 512


def row_moves(to):
    at = lambda y, h, c: (y * N_XH + h) * N_CORE + c
    return [(at(y, h, c), at(*to(y, h, c))) for y in range(N_Y) for h in range(N_XH) for c in range(N_CORE)]


def tensor_moves(to):
    at = lambda xl, z: xl * N_Z + z
    return [(at(xl, z), at(*to(xl, z))) for xl in range(N_XL) for z in range(N_Z)]


Y_UP = row_moves(lambda y, h, c: ((y + 1) % N_Y, h, c))
Y_DOWN = row_moves(lambda y, h, c: ((y - 1) % N_Y, h, c))
H_FLIP = row_moves(lambda y, h, c: (y, 1 - h, c))
C_FLIP = row_moves(lambda y, h, c: (y, h, 1 - c))
Z_UP = tensor_moves(lambda xl, z: (xl, (z + 1) % N_Z))
Z_DOWN = tensor_moves(lambda xl, z: (xl, (z - 1) % N_Z))
XL_FLIP = tensor_moves(lambda xl, z: (1 - xl, z))
BOTH_FLIP = [(r * N_XL * N_Z + t, r2 * N_XL * N_Z + t2) for r, r2 in H_FLIP for t, t2 in XL_FLIP]


def over_row(x, moves):
    return lax.ppermute(x, "row", moves)


def over_tensor(x, moves):
    return lax.ppermute(x, "tensor", moves)


def with_other_core(pieces):
    out = []
    for piece, (dy, dh), first in pieces:
        out.append((piece, (dy % N_Y, dh, 0), first))
        out.append((over_row(piece, C_FLIP), (dy % N_Y, dh, 1), first))
    return out


def y_pieces(own, dh):
    half = own.shape[0] // 2
    up = over_row(own, Y_UP)
    down = over_row(own, Y_DOWN)
    up2 = over_row(up[:half], Y_UP)
    down2 = over_row(down[half:], Y_DOWN)
    return [(own, (0, dh), 0), (up, (-1, dh), 0), (down, (1, dh), 0), (up2, (-2, dh), 0), (down2, (2, dh), half)]


def far_hidden(hidden, h, z):
    rows, depth = hidden.shape
    width = depth // (N_Y * N_XH)
    mine = lax.dynamic_slice_in_dim(hidden, (z * N_XH + 1 - h) * width, width, 1)
    mine = lax.ppermute(mine, ("row", "tensor"), BOTH_FLIP)
    half = rows // 2
    up = over_tensor(mine, Z_UP)
    down = over_tensor(mine, Z_DOWN)
    up2 = over_tensor(up[:half], Z_UP)
    down2 = over_tensor(down[half:], Z_DOWN)
    return [(mine, 0, 0), (down, 1, 0), (up, 3, 0), (up2, 2, 0), (down2, 2, half)]


def far_kernel(lefts, rights, place, *refs):
    n_left, n_right = len(lefts), len(rights)
    left_in, right_in, out = refs[:n_left], refs[n_left:n_left + n_right], refs[n_left + n_right]
    stack, right_buf, sems = refs[-3], refs[-2], refs[-1]
    copies, at = [], 0
    for i, (step, first) in enumerate(lefts):
        rows = left_in[i].shape[0]
        copies.append(pltpu.make_async_copy(left_in[i], stack.at[step, pl.ds(first, rows), :], sems.at[i]))
    begins = []
    for i in range(n_right):
        rows = right_in[i].shape[0]
        copies.append(pltpu.make_async_copy(right_in[i], right_buf.at[pl.ds(at, rows), :], sems.at[n_left + i]))
        begins.append(at)
        at += rows
    for copy in copies:
        copy.start()
    for copy in copies[:n_left]:
        copy.wait()
    for i, ((dy, _, dc), first) in enumerate(rights):
        rows = right_in[i].shape[0]
        copies[n_left + i].wait()
        column = pl.multiple_of(lax.rem(place[1] + dc, N_CORE) * DEPTH + first, DEPTH // 2)
        left = stack[lax.rem(place[0] + dy, N_Y), :, pl.ds(column, rows)]
        term = jnp.dot(left, right_buf[begins[i]:begins[i] + rows, :], preferred_element_type=jnp.float32)
        if i == 0:
            out[...] = term
        else:
            out[...] += term


def far_product(lefts, rights, place):
    left_arrays, right_arrays = [p[0] for p in lefts], [p[0] for p in rights]
    rows, width = left_arrays[0].shape
    depth, columns = sum(a.shape[0] for a in right_arrays), right_arrays[0].shape[1]
    anywhere = [pl.BlockSpec(memory_space=pl.ANY)] * (len(lefts) + len(rights))
    return pl.pallas_call(
        functools.partial(far_kernel, [p[1:] for p in lefts], [p[1:] for p in rights]),
        out_shape=jax.ShapeDtypeStruct((rows, columns), jnp.float32),
        in_specs=[pl.BlockSpec(memory_space=pltpu.SMEM)] + anywhere,
        out_specs=pl.BlockSpec(memory_space=pltpu.VMEM),
        scratch_shapes=[
            pltpu.VMEM((N_Y, rows, width), jnp.bfloat16),
            pltpu.VMEM((depth, columns), jnp.bfloat16),
            pltpu.SemaphoreType.DMA((len(lefts) + len(rights),)),
        ],
        name="far_product",
    )(place, *left_arrays, *right_arrays)


def project_kernel(blocks, apart, place, rows, *refs):
    count = sum(len(parts) for _, parts in blocks)
    pieces, refs = refs[:count], refs[count:]
    if apart:
        mine, other, total_buf, refs = refs[0], refs[1], refs[-2], refs[2:-2] + refs[-1:]
    else:
        total_buf, refs = refs[0], refs[1:]
    bufs, sems = refs[:-1], refs[-1]
    copies = [pltpu.make_async_copy(pieces[i], bufs[i], sems.at[i]) for i in range(count)]
    for copy in copies:
        copy.start()
    width = pieces[0].shape[1]
    i = 0
    for (dy, dh, dc), firsts in blocks:
        total = None
        for first in firsts:
            copies[i].wait()
            depth = pieces[i].shape[0]
            term = jnp.dot(rows[:, first:first + depth], bufs[i][...], preferred_element_type=jnp.float32)
            total = term if total is None else total + term
            i += 1
        group = lax.rem(place[0] + dy, N_Y) * N_XH + lax.rem(place[1] + dh, N_XH)
        to_xl = lax.rem(group // N_Z + place[3], N_XL)
        to_z = lax.rem(lax.rem(group, N_Z) + N_Z - place[4], N_Z)
        begin = pl.multiple_of(lax.rem(place[2] + dc, N_CORE) * width, width)
        total_buf[to_z, to_xl, :, pl.ds(begin, width)] = total.astype(jnp.bfloat16)
    if apart:
        mine[...] = total_buf[:, 0]
        other[...] = total_buf[:, 1]


def project(rows, pieces, place, groups, apart):
    by_block = {}
    for piece, shift, first in pieces:
        by_block.setdefault(shift, []).append((first, piece))
    blocks = tuple((shift, tuple(first for first, _ in parts)) for shift, parts in by_block.items())
    arrays = [piece for parts in by_block.values() for _, piece in parts]
    count, width = rows.shape[0], len(blocks) * arrays[0].shape[1] // groups
    vmem = pl.BlockSpec(memory_space=pltpu.VMEM)
    whole = (N_Z, N_XL, count, width)
    one = jax.ShapeDtypeStruct((N_Z, count, width), jnp.bfloat16)
    return pl.pallas_call(
        functools.partial(project_kernel, blocks, apart),
        out_shape=(one, one) if apart else jax.ShapeDtypeStruct(whole, jnp.bfloat16),
        in_specs=[pl.BlockSpec(memory_space=pltpu.SMEM), vmem] + [pl.BlockSpec(memory_space=pl.ANY)] * len(arrays),
        out_specs=(vmem, vmem) if apart else vmem,
        scratch_shapes=[pltpu.VMEM(a.shape, a.dtype) for a in arrays]
        + ([pltpu.VMEM(whole, jnp.bfloat16)] if apart else [])
        + [pltpu.SemaphoreType.DMA((len(arrays),))],
    )(place, rows, *arrays)


def member(row, shift):
    dy, dh, dc = shift
    y, h, c = row // (N_XH * N_CORE), (row // N_CORE) % N_XH, row % N_CORE
    return (((y + dy) % N_Y) * N_XH + (h ^ dh)) * N_CORE + (c ^ dc)


def attend_kernel(heads, first_tile, last, bounds, perm, q, offs, starts, k, vt, *refs):
    if last:
        perm_t, before, out, sorted_q, sorted_o, acc = refs
    else:
        out, sorted_q, acc = refs
        sorted_o = out
    tiles = offs.shape[0]
    lanes = heads * TILE
    chains = range(lanes // CHAIN)
    sorted_q[...] = jnp.dot(perm[...], q[...], preferred_element_type=jnp.float32).astype(jnp.bfloat16)
    sorted_o[...] = jnp.zeros_like(sorted_o)
    scale = math.log2(math.e) / math.sqrt(HEAD_SIZE)

    def tile(t, carry):
        lo, hi = bounds[0, first_tile + t], bounds[1, first_tile + t]

        @pl.when(hi > lo)
        def _():
            rows = pl.ds(pl.multiple_of(t * TILE, TILE), TILE)
            qt = jnp.concatenate([sorted_q[rows, pl.ds(h * HEAD_SIZE, HEAD_SIZE)] for h in range(heads)], axis=0)
            parts = [qt[c * CHAIN:(c + 1) * CHAIN] for c in chains]
            acc[...] = jnp.zeros_like(acc)

            def block(b, state):
                kb = k[pl.ds(pl.multiple_of(b * KB, KB), KB), :]
                key = b * KB + lax.broadcasted_iota(jnp.int32, (KB, CHAIN), 0)
                bias = jnp.where((key <= offs[t, :, :CHAIN]) & (key >= starts[t, :, :CHAIN]), 0.0, NEG)
                scores = [
                    lax.dot_general(kb, part, (((1,), (1,)), ((), ())), preferred_element_type=jnp.float32)
                    for part in parts
                ]
                new = []
                for c in chains:
                    top, total = state[c]
                    s = scores[c] * scale + bias
                    new_top = jnp.maximum(top, jnp.max(s, axis=0, keepdims=True))
                    p = jnp.exp2(s - new_top)
                    alpha = jnp.exp2(top - new_top)
                    cols = pl.ds(c * CHAIN, CHAIN)
                    acc[:, cols] = acc[:, cols] * alpha + jnp.dot(
                        vt[b], p.astype(jnp.bfloat16), preferred_element_type=jnp.float32
                    )
                    new.append((new_top, total * alpha + jnp.sum(p, axis=0, keepdims=True)))
                return tuple(new)

            init = tuple(
                (jnp.full((1, CHAIN), NEG, jnp.float32), jnp.zeros((1, CHAIN), jnp.float32)) for _ in chains
            )
            final = lax.fori_loop(lo, hi, block, init)
            total = jnp.concatenate([state[1] for state in final], axis=1)
            o = (acc[...] * (1.0 / total)).T.astype(jnp.bfloat16)
            for h in range(heads):
                sorted_o[rows, pl.ds(h * HEAD_SIZE, HEAD_SIZE)] = o[h * TILE:(h + 1) * TILE]

        return carry

    lax.fori_loop(0, tiles, tile, 0)
    if last:
        rows = jnp.concatenate([before[...], sorted_o[...]], axis=0)
        out[...] = jnp.dot(perm_t[...], rows, preferred_element_type=jnp.float32).astype(jnp.bfloat16)


def attend_tables(slot_offset, doc_lengths, heads):
    slots = slot_offset.shape[0]
    tiles = slots // TILE
    key = jnp.where(slot_offset < 0, 1 << 20, slot_offset)
    idx = jnp.arange(slots, dtype=jnp.int32)
    before = (key[None, :] < key[:, None]) | ((key[None, :] == key[:, None]) & (idx[None, :] < idx[:, None]))
    rank = jnp.sum(before.astype(jnp.int32), axis=1)
    perm = rank[None, :] == idx[:, None]
    perm_t = rank[:, None] == idx[None, :]
    offset = jnp.sum(jnp.where(perm, slot_offset[None, :], 0), axis=1)
    start, end = jnp.zeros_like(offset), 0
    for d in range(doc_lengths.shape[0]):
        end = end + doc_lengths[d] * 128
        start = jnp.where(offset >= end, end, start)
    tile_offset, tile_start = offset.reshape(tiles, TILE), start.reshape(tiles, TILE)
    top = jnp.max(tile_offset, axis=1)
    lo = jnp.where(top >= 0, tile_start[:, 0] // KB, 0)
    hi = jnp.where(top >= 0, top // KB + 1, 0)

    def spread(a):
        return jnp.broadcast_to(a[:, None, :], (tiles, heads, TILE)).reshape(tiles, 1, heads * TILE)

    return (
        jnp.stack([lo, hi]),
        perm.astype(jnp.bfloat16),
        perm_t.astype(jnp.bfloat16),
        spread(tile_offset),
        spread(tile_start),
    )


def attend_run(q, tables, k, vt, before, first_tile, last_tile):
    slots, width = q.shape
    heads = width // HEAD_SIZE
    bounds, perm, perm_t, offs, starts = tables
    last = before is not None
    rows = (last_tile - first_tile) * TILE
    run = slice(first_tile, last_tile)
    perm = perm[first_tile * TILE:last_tile * TILE]
    arrays = [bounds, perm, q, offs[run], starts[run], k, vt] + ([perm_t, before] if last else [])
    vmem = pl.BlockSpec(memory_space=pltpu.VMEM)
    buffers = [pltpu.VMEM((rows, width), jnp.bfloat16)] * (2 if last else 1)
    return pl.pallas_call(
        functools.partial(attend_kernel, heads, first_tile, last),
        out_shape=jax.ShapeDtypeStruct((slots if last else rows, width), jnp.bfloat16),
        in_specs=[pl.BlockSpec(memory_space=pltpu.SMEM)] + [vmem] * (len(arrays) - 1),
        out_specs=vmem,
        scratch_shapes=buffers + [pltpu.VMEM((HEAD_SIZE, heads * TILE), jnp.float32)],
    )(*arrays)


def attend(q, tables, k, vt):
    tiles = q.shape[0] // TILE
    cut = (tiles * 5 + 7) // 8
    before = attend_run(q, tables, k, vt, None, 0, cut)
    return attend_run(q, tables, k, vt, before, cut, tiles)


def exchange(x):
    return lax.all_to_all(x, "row", split_axis=0, concat_axis=0, tiled=True)


def added(a, b):
    return a.astype(jnp.float32) + b.astype(jnp.float32)


def rounded(a):
    return a.astype(jnp.bfloat16)


def reduce_z(part):
    half = part.shape[2] // 2
    mine, up1, far, down1 = part[0], part[1], part[2], part[3]
    far_up = over_tensor(far[:, :half], Z_UP)
    far_down = over_tensor(far[:, half:], Z_DOWN)
    up_b = over_tensor(up1[:, half:], Z_UP)
    down_a = over_tensor(down1[:, :half], Z_DOWN)
    up_a = over_tensor(rounded(added(up1[:, :half], far_up)), Z_UP)
    down_b = over_tensor(rounded(added(down1[:, half:], far_down)), Z_DOWN)
    top = added(mine[:, :half], down_a) + up_a.astype(jnp.float32)
    low = added(mine[:, half:], up_b) + down_b.astype(jnp.float32)
    return jnp.concatenate([top, low], axis=1)


def sublayer(hidden_rows, w_query, w_out, pack_key_cache, pack_value_cache, query_pos, doc_blocks):
    servers = lax.axis_size("row")
    groups = lax.axis_size("tensor")
    me = lax.axis_index("row")
    row_count = hidden_rows.shape[0]
    key_span = pack_key_cache.shape[0]
    capacity = 2 * row_count // servers
    slot_count = servers * capacity
    depth, head_width = w_query.shape
    heads = head_width // HEAD_SIZE

    server = query_pos // key_span
    idx = jnp.arange(row_count, dtype=jnp.int32)
    earlier = (server[None, :] == server[:, None]) & (idx[None, :] < idx[:, None])
    slot = server * capacity + jnp.sum(earlier.astype(jnp.int32), axis=1)
    in_slot = jnp.arange(slot_count, dtype=jnp.int32)[:, None] == slot[None, :]
    offset_out = jnp.sum(jnp.where(in_slot, (query_pos % key_span + 1)[None, :], 0), axis=1) - 1
    slot_offset = exchange(offset_out.reshape(servers, capacity)).reshape(slot_count)
    pack = in_slot.astype(jnp.bfloat16)
    unpack = (slot[:, None] == jnp.arange(slot_count, dtype=jnp.int32)[None, :]).astype(jnp.bfloat16)

    y, h, core = me // (N_XH * N_CORE), (me // N_CORE) % N_XH, me % N_CORE
    z = lax.axis_index("tensor") % N_Z
    far = far_hidden(hidden_rows, h, z)
    query_pieces = with_other_core(y_pieces(w_query, 0))
    far_queries = far_product(far, query_pieces, jnp.stack([(y + N_Z - z) % N_Y, core]))
    hidden_rows, far_queries = lax.optimization_barrier((hidden_rows, far_queries))
    queries = jnp.zeros((row_count, head_width), jnp.float32)
    for piece, shift, first in query_pieces:
        left = lax.dynamic_slice_in_dim(hidden_rows, member(me, shift) * depth + first, piece.shape[0], 1)
        queries = queries + jnp.dot(left, piece, preferred_element_type=jnp.float32)
    queries = rounded(queries + over_row(far_queries, H_FLIP))
    outgoing = rounded(jnp.dot(pack, queries, preferred_element_type=jnp.float32))
    slot_offset, pack_value_cache, outgoing = lax.optimization_barrier((slot_offset, pack_value_cache, outgoing))
    incoming = exchange(outgoing.reshape(servers, capacity, head_width)).reshape(slot_count, head_width)
    tables = attend_tables(slot_offset, doc_blocks[0], heads)
    vt = jnp.swapaxes(pack_value_cache.reshape(key_span // KB, KB, HEAD_SIZE), 1, 2)

    other_h = over_row(w_out, H_FLIP)
    out_pieces = with_other_core(y_pieces(w_out, 0) + y_pieces(other_h, 1))

    attended = attend(incoming, tables, pack_key_cache, vt)
    returned = exchange(attended.reshape(servers, capacity, head_width)).reshape(slot_count, head_width)
    half = row_count // 2
    rows_of = lambda part: rounded(jnp.dot(part, returned, preferred_element_type=jnp.float32))
    t = lax.axis_index("tensor")
    place = jnp.stack([y, h, core, t // N_Z, z])
    mine, other = project(rows_of(unpack[half:]), out_pieces, place, groups, True)
    other = over_tensor(other, XL_FLIP)
    first = project(rows_of(unpack[:half]), out_pieces, place, groups, False)
    first = reduce_z(first)
    first = rounded(added(first[0], over_tensor(rounded(first[1]), XL_FLIP)))
    second = rounded(reduce_z(rounded(added(mine, other))[:, None])[0])
    return jnp.concatenate([first, second], axis=0)


def solution(mesh):
    return jax.shard_map(
        sublayer,
        mesh=mesh,
        in_specs=(
            P("row", None),
            P("row", "tensor"),
            P("tensor", "row"),
            P("row", "tensor"),
            P("row", "tensor"),
            P("row"),
            P("row", None),
        ),
        out_specs=P("row", "tensor"),
        check_vma=False,
    )
```

profile of v0, /device:TPU:1, one launch (start us, length us, event | category | flops | bytes accessed | tf_op | source)
XLA Modules:
  0.0 283.2 jit_solution(1952591390141517754)
XLA Ops:
  1.1 3.4 %collective-permute-start = (bf16[256,1024]{1,0:T(8,128)(2,1)S(1)}, bf16[256,1024]{1,0:T(8,128)(2,1)S(1)}, u32[]{:S(2)}, u32[]{:S(2)}) collective-permute-start(bf16[256,1024]{1,0:T(8,128)(2,1)S(1)} %constant_dynamic-slice_fusion), channel_id=1, source_target_pairs={{0,20},{1,21},{2,22},{3,23},{4,16},{5,17},{6,18},{7,19},{8,28},{9,... | collective-permute-start | bytes 1572872 | tf_op jit(solution)/shard_map/ppermute | solution.py:71
  7.2 8.6 %collective-permute-done.refs_0_ = bf16[256,1024]{1,0:T(8,128)(2,1)S(1)} collective-permute-done((bf16[256,1024]{1,0:T(8,128)(2,1)S(1)}, bf16[256,1024]{1,0:T(8,128)(2,1)S(1)}, u32[]{:S(2)}, u32[]{:S(2)}) %collective-permute-start) | collective-permute-done | bytes 524320 | tf_op jit(solution)/shard_map/ppermute | solution.py:71
  15.8 4.0 %collective-permute-start.1 = (bf16[256,1024]{1,0:T(8,128)(2,1)S(1)}, bf16[256,1024]{1,0:T(8,128)(2,1)S(1)}, u32[]{:S(2)}, u32[]{:S(2)}) collective-permute-start(bf16[256,1024]{1,0:T(8,128)(2,1)S(1)} %collective-permute-done.refs_0_), channel_id=1, source_target_pairs={{0,3},{1,0},{2,1},{3,2},{4,7},{5,4},{6,5},{7,6},{8,11},{9,8},{10,9... | collective-permute-start | bytes 1572872 | tf_op jit(solution)/shard_map/ppermute | solution.py:47
  22.9 6.9 %collective-permute-done.1.refs_1_ = bf16[256,1024]{1,0:T(8,128)(2,1)S(1)} collective-permute-done((bf16[256,1024]{1,0:T(8,128)(2,1)S(1)}, bf16[256,1024]{1,0:T(8,128)(2,1)S(1)}, u32[]{:S(2)}, u32[]{:S(2)}) %collective-permute-start.1) | collective-permute-done | bytes 524320 | tf_op jit(solution)/shard_map/ppermute | solution.py:47
  35.7 11.3 %collective-permute-done.2.refs_2_ = bf16[256,1024]{1,0:T(8,128)(2,1)S(1)} collective-permute-done((bf16[256,1024]{1,0:T(8,128)(2,1)S(1)}, bf16[256,1024]{1,0:T(8,128)(2,1)S(1)}, u32[]{:S(2)}, u32[]{:S(2)}) %collective-permute-start.2) | collective-permute-done | bytes 524320 | tf_op jit(solution)/shard_map/ppermute | solution.py:47
  55.4 3.4 %collective-permute-start.9 = (bf16[512,1024]{1,0:T(8,128)(2,1)S(1)}, bf16[512,1024]{1,0:T(8,128)(2,1)}, u32[]{:S(2)}, u32[]{:S(2)}) collective-permute-start(bf16[512,1024]{1,0:T(8,128)(2,1)S(1)} %collective-permute-done.8.refs_9_), channel_id=1, source_target_pairs={{0,8},{8,0},{16,24},{24,16},{32,40},{40,32},{48,56},{56,48},{64,72... | collective-permute-start | bytes 3145736 | tf_op jit(solution)/shard_map/ppermute | solution.py:43
  60.0 3.6 %collective-permute-done.10.refs_11_ = bf16[256,1024]{1,0:T(8,128)(2,1)} collective-permute-done((bf16[256,1024]{1,0:T(8,128)(2,1)S(1)}, bf16[256,1024]{1,0:T(8,128)(2,1)}, u32[]{:S(2)}, u32[]{:S(2)}) %collective-permute-start.10) | collective-permute-done | bytes 524320 | tf_op jit(solution)/shard_map/ppermute | solution.py:43
  72.1 7.0 %all-to-all-start = ((s32[16,1,32]{2,1,0:T(1,128)}), s32[16,1,32]{2,1,0:T(1,128)S(1)}, u32[]{:S(2)}, u32[]{:S(2)}) async-start(s32[16,1,32]{2,1,0:T(1,128)} %sub.60), calls=%async_computation | async-start | bytes 16384 | tf_op jit(solution)/shard_map/all_to_all | solution.py:308
  83.0 3.1 %all-to-all-done = s32[16,1,32]{2,1,0:T(1,128)S(1)} async-done(((s32[16,1,32]{2,1,0:T(1,128)}), s32[16,1,32]{2,1,0:T(1,128)S(1)}, u32[]{:S(2)}, u32[]{:S(2)}) %all-to-all-start) | async-done | bytes 2080 | tf_op jit(solution)/shard_map/all_to_all | solution.py:308
  92.4 6.5 %far_product.1 = f32[256,1024]{1,0:T(8,128)} custom-call(s32[2]{0:T(128)} %pad_add_fusion.1.place, bf16[256,1024]{1,0:T(8,128)(2,1)} %copy-done.12, bf16[256,1024]{1,0:T(8,128)(2,1)} %copy-done.9, bf16[256,1024]{1,0:T(8,128)(2,1)} %copy-done.10, bf16[128,1024]{1,0:T(8,128)(2,1)} %copy-done.13, bf16[128,1024]{1,0:T(8,128)(2,1)} %collective-permute-done.4.refs_4_, ...), custom_call_target="tpu_custom_call" | custom-call | tf_op jit(solution)/shard_map/far_product/pallas_call | solution.py:115
  113.7 11.4 %collective-permute-done.14 = f32[256,1024]{1,0:T(8,128)} collective-permute-done((f32[256,1024]{1,0:T(8,128)}, f32[256,1024]{1,0:T(8,128)}, u32[]{:S(2)}, u32[]{:S(2)}) %collective-permute-start.14) | collective-permute-done | bytes 1048608 | tf_op jit(solution)/shard_map/ppermute | solution.py:43
  127.5 3.1 %convolution_convert_fusion = bf16[512,1024]{1,0:T(8,128)(2,1)} fusion(f32[256,1024]{1,0:T(8,128)} %collective-permute-done.14, f32[256,1024]{1,0:T(8,128)S(1)} %fusion.1, bf16[256,1024]{1,0:T(8,128)(2,1)} %collective-permute-done.13.refs_14_, s32[256]{0:T(256)S(1)} %multiply_add_fusion, bf16[256,8192]{1,0:T(8,128)(2,1)} %param.7, s32[]{:T(128)S(6)} %select_n.298), kind=kOutput, calls=%fused_computation.1 | convolution fusion | flops 404094976 | bytes 3802116 | tf_op jit(solution)/shard_map/dot_general | solution.py:365
  132.0 5.5 %all-to-all-start.1 = ((bf16[16,32,1024]{2,1,0:T(8,128)(2,1)}), bf16[16,32,1024]{2,1,0:T(8,128)(2,1)S(1)}, u32[]{:S(2)}, u32[]{:S(2)}) async-start(bf16[16,32,1024]{2,1,0:T(8,128)(2,1)} %bitcast.76), calls=%async_computation.1 | async-start | bytes 2097152 | tf_op jit(solution)/shard_map/all_to_all | solution.py:308
  143.0 3.9 %copy.10 = bf16[8,1024,128]{1,2,0:T(8,128)(2,1)} copy(bf16[8,1024,128]{2,1,0:T(8,128)(2,1)} %bitcast.78) | data formatting | bytes 4194304 | tf_op jit(solution)/shard_map/reshape | solution.py:369
  149.3 5.3 %collective-permute-done.28.refs_14_ = bf16[1024,512]{1,0:T(8,128)(2,1)} collective-permute-done((bf16[1024,512]{1,0:T(8,128)(2,1)}, bf16[1024,512]{1,0:T(8,128)(2,1)}, u32[]{:S(2)}, u32[]{:S(2)}) %collective-permute-start.28) | collective-permute-done | bytes 1048608 | tf_op jit(solution)/shard_map/ppermute | solution.py:43
  154.6 6.4 %collective-permute-start.23 = (bf16[512,512]{1,0:T(8,128)(2,1)}, bf16[512,512]{1,0:T(8,128)(2,1)}, u32[]{:S(2)}, u32[]{:S(2)}) collective-permute-start(bf16[512,512]{1,0:T(8,128)(2,1)} %collective-permute-done.21.refs_7_), channel_id=1, source_target_pairs={{0,8},{8,0},{16,24},{24,16},{32,40},{40,32},{48,56},{56,48},{64,72... | collective-permute-start | bytes 1572872 | tf_op jit(solution)/shard_map/ppermute | solution.py:43
  162.5 21.7 %shard_map.73.refs_1_ = bf16[320,1024]{1,0:T(8,128)(2,1)} custom-call(s32[2,8]{1,0:T(2,128)} %pad_add_fusion.bounds, bf16[320,512]{1,0:T(8,128)(2,1)} %slice.249.perm, bf16[512,1024]{1,0:T(8,128)(2,1)} %bitcast.74, s32[5,1,512]{2,1,0:T(1,128)} %slice.210.offs, s32[5,1,512]{2,1,0:T(1,128)} %slice.213.starts, bf16[8192,128]{1,0:T(8,128)(2,1)} %k.3, ...), custom_call_target="tpu_custom_call" | custom-call | tf_op jit(solution)/shard_map/pallas_call | solution.py:291
  184.3 5.1 %shard_map.74 = bf16[512,1024]{1,0:T(8,128)(2,1)} custom-call(s32[2,8]{1,0:T(2,128)} %pad_add_fusion.bounds, bf16[192,512]{1,0:T(8,128)(2,1)} %slice.248.perm, bf16[512,1024]{1,0:T(8,128)(2,1)} %bitcast.75, s32[3,1,512]{2,1,0:T(1,128)} %slice.203.offs, s32[3,1,512]{2,1,0:T(1,128)} %slice.206.starts, bf16[8192,128]{1,0:T(8,128)(2,1)} %k.3, ...), custom_call_target="tpu_custom_call" | custom-call | tf_op jit(solution)/shard_map/pallas_call | solution.py:291
  189.4 8.5 %all-to-all-start.2 = ((bf16[16,32,1024]{2,1,0:T(8,128)(2,1)}), bf16[16,32,1024]{2,1,0:T(8,128)(2,1)S(1)}, u32[]{:S(2)}, u32[]{:S(2)}) async-start(bf16[16,32,1024]{2,1,0:T(8,128)(2,1)} %bitcast.77), calls=%async_computation.2 | async-start | bytes 2097152 | tf_op jit(solution)/shard_map/all_to_all | solution.py:308
  204.0 19.9 %collective-permute-done.30.refs_16_ = bf16[512,512]{1,0:T(8,128)(2,1)} collective-permute-done((bf16[512,512]{1,0:T(8,128)(2,1)S(1)}, bf16[512,512]{1,0:T(8,128)(2,1)}, u32[]{:S(2)}, u32[]{:S(2)}) %collective-permute-start.30) | collective-permute-done | bytes 524320 | tf_op jit(solution)/shard_map/ppermute | solution.py:43
  229.1 9.0 %shard_map.76 = (bf16[4,128,1024]{2,1,0:T(8,128)(2,1)}, bf16[4,128,1024]{2,1,0:T(8,128)(2,1)}) custom-call(s32[5]{0:T(128)} %stack.35.place, bf16[128,1024]{1,0:T(8,128)(2,1)} %convolution_convert_fusion.1.rows, bf16[1024,512]{1,0:T(8,128)(2,1)} %refs_0_.3, bf16[1024,512]{1,0:T(8,128)(2,1)} %collective-permute-done.15.refs_1_, bf16[1024,512]{1,0:T(8,128)(2,1)} %copy-done.1, ...), custom_call_target="tpu_custom_call" | custom-call | tf_op jit(solution)/shard_map/pallas_call | solution.py:170
  239.6 8.9 %shard_map.75 = bf16[4,2,128,1024]{3,2,1,0:T(8,128)(2,1)} custom-call(s32[5]{0:T(128)} %stack.35.place, bf16[128,1024]{1,0:T(8,128)(2,1)} %convolution_convert_fusion.2.rows, bf16[1024,512]{1,0:T(8,128)(2,1)} %refs_0_.3, bf16[1024,512]{1,0:T(8,128)(2,1)} %collective-permute-done.15.refs_1_, bf16[1024,512]{1,0:T(8,128)(2,1)} %copy-done.1, ...), custom_call_target="tpu_custom_call" | custom-call | tf_op jit(solution)/shard_map/pallas_call | solution.py:170
  259.3 3.3 %collective-permute-done.41 = bf16[4,128,1024]{2,1,0:T(8,128)(2,1)S(1)} collective-permute-done((bf16[4,128,1024]{2,1,0:T(8,128)(2,1)}, bf16[4,128,1024]{2,1,0:T(8,128)(2,1)S(1)}, u32[]{:S(2)}, u32[]{:S(2)}) %collective-permute-start.41) | collective-permute-done | bytes 1048608 | tf_op jit(solution)/shard_map/ppermute | solution.py:47
  264.5 4.3 %collective-permute-done.39 = bf16[2,64,1024]{2,1,0:T(8,128)(2,1)S(1)} collective-permute-done((bf16[2,64,1024]{2,1,0:T(8,128)(2,1)S(1)}, bf16[2,64,1024]{2,1,0:T(8,128)(2,1)S(1)}, u32[]{:S(2)}, u32[]{:S(2)}) %collective-permute-start.39) | collective-permute-done | bytes 262176 | tf_op jit(solution)/shard_map/ppermute | solution.py:47
  (190 shorter events, 106.1 us)
Async XLA Ops:
  4.5 27.8 %collective-permute-start.6 = (bf16[512,1024]{1,0:T(8,128)(2,1)}, bf16[512,1024]{1,0:T(8,128)(2,1)}, u32[]{:S(2)}, u32[]{:S(2)}) collective-permute-start(bf16[512,1024]{1,0:T(8,128)(2,1)} %refs_5_.1), channel_id=1, source_target_pairs={{0,32},{8,40},{16,48},{24,56},{32,64},{40,72},{48,80},{56,88},{64,... | collective-permute-start | bytes 3145736 | tf_op jit(solution)/shard_map/ppermute | solution.py:43
  5.8 28.2 %collective-permute-start.8 = (bf16[512,1024]{1,0:T(8,128)(2,1)}, bf16[512,1024]{1,0:T(8,128)(2,1)S(1)}, u32[]{:S(2)}, u32[]{:S(2)}) collective-permute-start(bf16[512,1024]{1,0:T(8,128)(2,1)} %refs_5_.1), channel_id=1, source_target_pairs={{0,96},{8,104},{16,112},{24,120},{32,0},{40,8},{48,16},{56,24},{64... | collective-permute-start | bytes 3145736 | tf_op jit(solution)/shard_map/ppermute | solution.py:43
  19.9 27.1 %collective-permute-start.5 = (bf16[512,1024]{1,0:T(8,128)(2,1)}, bf16[512,1024]{1,0:T(8,128)(2,1)S(1)}, u32[]{:S(2)}, u32[]{:S(2)}) collective-permute-start(bf16[512,1024]{1,0:T(8,128)(2,1)} %refs_5_.1), channel_id=1, source_target_pairs={{0,8},{8,0},{16,24},{24,16},{32,40},{40,32},{48,56},{56,48},{64,72... | collective-permute-start | bytes 3145736 | tf_op jit(solution)/shard_map/ppermute | solution.py:43
  21.6 30.8 %collective-permute-start.16 = (bf16[1024,512]{1,0:T(8,128)(2,1)}, bf16[1024,512]{1,0:T(8,128)(2,1)S(1)}, u32[]{:S(2)}, u32[]{:S(2)}) collective-permute-start(bf16[1024,512]{1,0:T(8,128)(2,1)} %refs_0_.3), channel_id=1, source_target_pairs={{0,32},{8,40},{16,48},{24,56},{32,64},{40,72},{48,80},{56,88},{64,... | collective-permute-start | bytes 3145736 | tf_op jit(solution)/shard_map/ppermute | solution.py:43
  29.7 25.6 %collective-permute-start.18 = (bf16[1024,512]{1,0:T(8,128)(2,1)}, bf16[1024,512]{1,0:T(8,128)(2,1)S(1)}, u32[]{:S(2)}, u32[]{:S(2)}) collective-permute-start(bf16[1024,512]{1,0:T(8,128)(2,1)} %refs_0_.3), channel_id=1, source_target_pairs={{0,96},{8,104},{16,112},{24,120},{32,0},{40,8},{48,16},{56,24},{64... | collective-permute-start | bytes 3145736 | tf_op jit(solution)/shard_map/ppermute | solution.py:43
  32.3 27.4 %collective-permute-start.24 = (bf16[1024,512]{1,0:T(8,128)(2,1)}, bf16[1024,512]{1,0:T(8,128)(2,1)}, u32[]{:S(2)}, u32[]{:S(2)}) collective-permute-start(bf16[1024,512]{1,0:T(8,128)(2,1)} %refs_0_.3), channel_id=1, source_target_pairs={{0,16},{8,24},{16,0},{24,8},{32,48},{40,56},{48,32},{56,40},{64,80... | collective-permute-start | bytes 3145736 | tf_op jit(solution)/shard_map/ppermute | solution.py:43
  52.4 37.4 %collective-permute-start.7 = (bf16[512,1024]{1,0:T(8,128)(2,1)}, bf16[512,1024]{1,0:T(8,128)(2,1)}, u32[]{:S(2)}, u32[]{:S(2)}) collective-permute-start(bf16[512,1024]{1,0:T(8,128)(2,1)} %collective-permute-done.6.refs_7_), channel_id=1, source_target_pairs={{0,8},{8,0},{16,24},{24,16},{32,40},{40,32},{48,56},{56,48},{64,72... | collective-permute-start | bytes 3145736 | tf_op jit(solution)/shard_map/ppermute | solution.py:43
  55.4 34.7 %collective-permute-start.9 = (bf16[512,1024]{1,0:T(8,128)(2,1)S(1)}, bf16[512,1024]{1,0:T(8,128)(2,1)}, u32[]{:S(2)}, u32[]{:S(2)}) collective-permute-start(bf16[512,1024]{1,0:T(8,128)(2,1)S(1)} %collective-permute-done.8.refs_9_), channel_id=1, source_target_pairs={{0,8},{8,0},{16,24},{24,16},{32,40},{40,32},{48,56},{56,48},{64,72... | collective-permute-start | bytes 3145736 | tf_op jit(solution)/shard_map/ppermute | solution.py:43
  63.6 28.8 %collective-permute-start.11 = (bf16[256,1024]{1,0:T(8,128)(2,1)}, bf16[256,1024]{1,0:T(8,128)(2,1)}, u32[]{:S(2)}, u32[]{:S(2)}) collective-permute-start(bf16[256,1024]{1,0:T(8,128)(2,1)} %collective-permute-done.10.refs_11_), channel_id=1, source_target_pairs={{0,8},{8,0},{16,24},{24,16},{32,40},{40,32},{48,56},{56,48},{64,72... | collective-permute-start | bytes 1572872 | tf_op jit(solution)/shard_map/ppermute | solution.py:43
  65.3 27.1 %collective-permute-start.13 = (bf16[256,1024]{1,0:T(8,128)(2,1)}, bf16[256,1024]{1,0:T(8,128)(2,1)}, u32[]{:S(2)}, u32[]{:S(2)}) collective-permute-start(bf16[256,1024]{1,0:T(8,128)(2,1)} %collective-permute-done.12.refs_13_), channel_id=1, source_target_pairs={{0,8},{8,0},{16,24},{24,16},{32,40},{40,32},{48,56},{56,48},{64,72... | collective-permute-start | bytes 1572872 | tf_op jit(solution)/shard_map/ppermute | solution.py:43
  89.2 110.8 %collective-permute-start.15 = (bf16[1024,512]{1,0:T(8,128)(2,1)}, bf16[1024,512]{1,0:T(8,128)(2,1)}, u32[]{:S(2)}, u32[]{:S(2)}) collective-permute-start(bf16[1024,512]{1,0:T(8,128)(2,1)} %refs_0_.3), channel_id=1, source_target_pairs={{0,8},{8,0},{16,24},{24,16},{32,40},{40,32},{48,56},{56,48},{64,72... | collective-permute-start | bytes 3145736 | tf_op jit(solution)/shard_map/ppermute | solution.py:43
  89.7 52.2 %collective-permute-start.20 = (bf16[512,512]{1,0:T(8,128)(2,1)}, bf16[512,512]{1,0:T(8,128)(2,1)}, u32[]{:S(2)}, u32[]{:S(2)}) collective-permute-start(bf16[512,512]{1,0:T(8,128)(2,1)} %slice.250), channel_id=1, source_target_pairs={{0,32},{8,40},{16,48},{24,56},{32,64},{40,72},{48,80},{56,88},{64,... | collective-permute-start | bytes 1572872 | tf_op jit(solution)/shard_map/ppermute | solution.py:43
  90.0 58.4 %collective-permute-start.21 = (bf16[512,512]{1,0:T(8,128)(2,1)}, bf16[512,512]{1,0:T(8,128)(2,1)}, u32[]{:S(2)}, u32[]{:S(2)}) collective-permute-start(bf16[512,512]{1,0:T(8,128)(2,1)} %slice.251), channel_id=1, source_target_pairs={{0,96},{8,104},{16,112},{24,120},{32,0},{40,8},{48,16},{56,24},{64... | collective-permute-start | bytes 1572872 | tf_op jit(solution)/shard_map/ppermute | solution.py:43
  92.4 56.6 %collective-permute-start.26 = (bf16[1024,512]{1,0:T(8,128)(2,1)}, bf16[1024,512]{1,0:T(8,128)(2,1)}, u32[]{:S(2)}, u32[]{:S(2)}) collective-permute-start(bf16[1024,512]{1,0:T(8,128)(2,1)} %collective-permute-done.24.refs_10_), channel_id=1, source_target_pairs={{0,32},{8,40},{16,48},{24,56},{32,64},{40,72},{48,80},{56,88},{64,... | collective-permute-start | bytes 3145736 | tf_op jit(solution)/shard_map/ppermute | solution.py:43
  98.9 26.2 %collective-permute-start.14 = (f32[256,1024]{1,0:T(8,128)}, f32[256,1024]{1,0:T(8,128)}, u32[]{:S(2)}, u32[]{:S(2)}) collective-permute-start(f32[256,1024]{1,0:T(8,128)} %far_product.1), channel_id=1, source_target_pairs={{0,16},{8,24},{16,0},{24,8},{32,48},{40,56},{48,32},{56,40},{64,80... | collective-permute-start | bytes 3145736 | tf_op jit(solution)/shard_map/ppermute | solution.py:43
  125.1 29.5 %collective-permute-start.28 = (bf16[1024,512]{1,0:T(8,128)(2,1)}, bf16[1024,512]{1,0:T(8,128)(2,1)}, u32[]{:S(2)}, u32[]{:S(2)}) collective-permute-start(bf16[1024,512]{1,0:T(8,128)(2,1)} %collective-permute-done.24.refs_10_), channel_id=1, source_target_pairs={{0,96},{8,104},{16,112},{24,120},{32,0},{40,8},{48,16},{56,24},{64... | collective-permute-start | bytes 3145736 | tf_op jit(solution)/shard_map/ppermute | solution.py:43
  132.0 29.6 %all-to-all-start.1 = ((bf16[16,32,1024]{2,1,0:T(8,128)(2,1)}), bf16[16,32,1024]{2,1,0:T(8,128)(2,1)S(1)}, u32[]{:S(2)}, u32[]{:S(2)}) async-start(bf16[16,32,1024]{2,1,0:T(8,128)(2,1)} %bitcast.76), calls=%async_computation.1 | async-start | bytes 2097152 | tf_op jit(solution)/shard_map/all_to_all | solution.py:308
  141.9 59.5 %collective-permute-start.17 = (bf16[1024,512]{1,0:T(8,128)(2,1)S(1)}, bf16[1024,512]{1,0:T(8,128)(2,1)}, u32[]{:S(2)}, u32[]{:S(2)}) collective-permute-start(bf16[1024,512]{1,0:T(8,128)(2,1)S(1)} %collective-permute-done.16.refs_2_), channel_id=1, source_target_pairs={{0,8},{8,0},{16,24},{24,16},{32,40},{40,32},{48,56},{56,48},{64,72... | collective-permute-start | bytes 3145736 | tf_op jit(solution)/shard_map/ppermute | solution.py:43
  148.4 54.3 %collective-permute-start.19 = (bf16[1024,512]{1,0:T(8,128)(2,1)S(1)}, bf16[1024,512]{1,0:T(8,128)(2,1)}, u32[]{:S(2)}, u32[]{:S(2)}) collective-permute-start(bf16[1024,512]{1,0:T(8,128)(2,1)S(1)} %collective-permute-done.18.refs_4_), channel_id=1, source_target_pairs={{0,8},{8,0},{16,24},{24,16},{32,40},{40,32},{48,56},{56,48},{64,72... | collective-permute-start | bytes 3145736 | tf_op jit(solution)/shard_map/ppermute | solution.py:43
  149.0 54.4 %collective-permute-start.22 = (bf16[512,512]{1,0:T(8,128)(2,1)}, bf16[512,512]{1,0:T(8,128)(2,1)}, u32[]{:S(2)}, u32[]{:S(2)}) collective-permute-start(bf16[512,512]{1,0:T(8,128)(2,1)} %collective-permute-done.20.refs_6_), channel_id=1, source_target_pairs={{0,8},{8,0},{16,24},{24,16},{32,40},{40,32},{48,56},{56,48},{64,72... | collective-permute-start | bytes 1572872 | tf_op jit(solution)/shard_map/ppermute | solution.py:43
  154.6 48.9 %collective-permute-start.23 = (bf16[512,512]{1,0:T(8,128)(2,1)}, bf16[512,512]{1,0:T(8,128)(2,1)}, u32[]{:S(2)}, u32[]{:S(2)}) collective-permute-start(bf16[512,512]{1,0:T(8,128)(2,1)} %collective-permute-done.21.refs_7_), channel_id=1, source_target_pairs={{0,8},{8,0},{16,24},{24,16},{32,40},{40,32},{48,56},{56,48},{64,72... | collective-permute-start | bytes 1572872 | tf_op jit(solution)/shard_map/ppermute | solution.py:43
  189.4 36.3 %all-to-all-start.2 = ((bf16[16,32,1024]{2,1,0:T(8,128)(2,1)}), bf16[16,32,1024]{2,1,0:T(8,128)(2,1)S(1)}, u32[]{:S(2)}, u32[]{:S(2)}) async-start(bf16[16,32,1024]{2,1,0:T(8,128)(2,1)} %bitcast.77), calls=%async_computation.2 | async-start | bytes 2097152 | tf_op jit(solution)/shard_map/all_to_all | solution.py:308
  202.8 25.0 %collective-permute-start.25 = (bf16[1024,512]{1,0:T(8,128)(2,1)}, bf16[1024,512]{1,0:T(8,128)(2,1)S(1)}, u32[]{:S(2)}, u32[]{:S(2)}) collective-permute-start(bf16[1024,512]{1,0:T(8,128)(2,1)} %collective-permute-done.24.refs_10_), channel_id=1, source_target_pairs={{0,8},{8,0},{16,24},{24,16},{32,40},{40,32},{48,56},{56,48},{64,72... | collective-permute-start | bytes 3145736 | tf_op jit(solution)/shard_map/ppermute | solution.py:43
  238.1 24.5 %collective-permute-start.41 = (bf16[4,128,1024]{2,1,0:T(8,128)(2,1)}, bf16[4,128,1024]{2,1,0:T(8,128)(2,1)S(1)}, u32[]{:S(2)}, u32[]{:S(2)}) collective-permute-start(bf16[4,128,1024]{2,1,0:T(8,128)(2,1)} %get-tuple-element.18), channel_id=1, source_target_pairs={{0,4},{1,5},{2,6},{3,7},{4,0},{5,1},{6,2},{7,3},{8,12},{9,13},{10,... | collective-permute-start | bytes 3145736 | tf_op jit(solution)/shard_map/ppermute | solution.py:47
  (42 other events, 816.5 us)
where the time goes:
time: 288 us; the launch traced here: 283 us
  waiting for transfers between devices  98 us (34%)
  starting transfers between devices  80.5 us (28%)
  Pallas kernels  51.2 us (18%)
  local copies, waits for them, and re-layouts  24.3 us (8%)
  matrix products  19.2 us (7%)
  other arithmetic  6.77 us (2%)
  between operations  3.13 us (1%)
    ppermute x18, waiting for transfers between devices, over_tensor(): return lax.ppermute(x, 'tensor', moves)  43.4 us
    ppermute x29, waiting for transfers between devices, over_row(): return lax.ppermute(x, 'row', moves)  42.9 us
    ppermute x29, starting transfers between devices, over_row(): return lax.ppermute(x, 'row', moves)  40.9 us
    pallas_call x2, Pallas kernels, attend_run(): pl.pallas_call(functools.partial(attend_kernel, heads, first_tile, last),...  26.8 us
    all_to_all x3, starting transfers between devices, exchange(): return lax.all_to_all(x, 'row', split_axis=0, concat_axis=0, tiled=True)  20.9 us
    pallas_call x2, Pallas kernels, project(): pl.pallas_call(functools.partial(project_kernel, blocks, apart), out_shap...  18 us
    ppermute x18, starting transfers between devices, over_tensor(): return lax.ppermute(x, 'tensor', moves)  15.3 us
    dot_general x9, matrix products, sublayer(): queries = queries + jnp.dot(left, piece, preferred_element_type=jnp.float32)  14.2 us
  transfers between devices with their start and end apart: 51, of which 22 were waited for; matrix products, arithmetic and copies ran while one was open for 16% of the time, Pallas kernels for 15%

commit v1 on v0

--- a/solution.py
+++ b/solution.py
@@ -77,27 +77,33 @@
     return [(mine, 0, 0), (down, 1, 0), (up, 3, 0), (up2, 2, 0), (down2, 2, half)]
 
 
-def far_kernel(lefts, rights, place, *refs):
-    n_left, n_right = len(lefts), len(rights)
+def part_kernel(lefts, rights, place, *refs):
+    n_left, n_right = max(len(lefts), 1), len(rights)
     left_in, right_in, out = refs[:n_left], refs[n_left:n_left + n_right], refs[n_left + n_right]
     stack, right_buf, sems = refs[-3], refs[-2], refs[-1]
     copies, at = [], 0
     for i, (step, first) in enumerate(lefts):
         rows = left_in[i].shape[0]
         copies.append(pltpu.make_async_copy(left_in[i], stack.at[step, pl.ds(first, rows), :], sems.at[i]))
+    n_copies = len(lefts) or N_Y
+    if not lefts:
+        width = stack.shape[2]
+        for step in range(N_Y):
+            column = pl.multiple_of((step * N_XH + place[2]) * width, width)
+            copies.append(pltpu.make_async_copy(left_in[0].at[:, pl.ds(column, width)], stack.at[step], sems.at[step]))
     begins = []
     for i in range(n_right):
         rows = right_in[i].shape[0]
-        copies.append(pltpu.make_async_copy(right_in[i], right_buf.at[pl.ds(at, rows), :], sems.at[n_left + i]))
+        copies.append(pltpu.make_async_copy(right_in[i], right_buf.at[pl.ds(at, rows), :], sems.at[n_copies + i]))
         begins.append(at)
         at += rows
     for copy in copies:
         copy.start()
-    for copy in copies[:n_left]:
+    for copy in copies[:n_copies]:
         copy.wait()
     for i, ((dy, _, dc), first) in enumerate(rights):
         rows = right_in[i].shape[0]
-        copies[n_left + i].wait()
+        copies[n_copies + i].wait()
         column = pl.multiple_of(lax.rem(place[1] + dc, N_CORE) * DEPTH + first, DEPTH // 2)
         left = stack[lax.rem(place[0] + dy, N_Y), :, pl.ds(column, rows)]
         term = jnp.dot(left, right_buf[begins[i]:begins[i] + rows, :], preferred_element_type=jnp.float32)
@@ -107,22 +113,22 @@
             out[...] += term
 
 
-def far_product(lefts, rights, place):
-    left_arrays, right_arrays = [p[0] for p in lefts], [p[0] for p in rights]
-    rows, width = left_arrays[0].shape
+def part_product(lefts, rights, place, whole=None):
+    left_arrays, right_arrays = [p[0] for p in lefts] or [whole], [p[0] for p in rights]
+    rows, width = left_arrays[0].shape[0], DEPTH * N_CORE
     depth, columns = sum(a.shape[0] for a in right_arrays), right_arrays[0].shape[1]
-    anywhere = [pl.BlockSpec(memory_space=pl.ANY)] * (len(lefts) + len(rights))
+    anywhere = [pl.BlockSpec(memory_space=pl.ANY)] * (len(left_arrays) + len(rights))
     return pl.pallas_call(
-        functools.partial(far_kernel, [p[1:] for p in lefts], [p[1:] for p in rights]),
+        functools.partial(part_kernel, [p[1:] for p in lefts], [p[1:] for p in rights]),
         out_shape=jax.ShapeDtypeStruct((rows, columns), jnp.float32),
-        in_specs=[pl.BlockSpec(memory_space=pltpu.SMEM)] + anywhere,
+        in_specs=[pl.BlockSpec(memory_space=pltpu.SMEM)]
+        + anywhere,
         out_specs=pl.BlockSpec(memory_space=pltpu.VMEM),
         scratch_shapes=[
             pltpu.VMEM((N_Y, rows, width), jnp.bfloat16),
             pltpu.VMEM((depth, columns), jnp.bfloat16),
-            pltpu.SemaphoreType.DMA((len(lefts) + len(rights),)),
+            pltpu.SemaphoreType.DMA(((len(lefts) or N_Y) + len(rights),)),
         ],
-        name="far_product",
     )(place, *left_arrays, *right_arrays)
 
 
@@ -178,12 +184,6 @@
     )(place, rows, *arrays)
 
 
-def member(row, shift):
-    dy, dh, dc = shift
-    y, h, c = row // (N_XH * N_CORE), (row // N_CORE) % N_XH, row % N_CORE
-    return (((y + dy) % N_Y) * N_XH + (h ^ dh)) * N_CORE + (c ^ dc)
-
-
 def attend_kernel(heads, first_tile, last, bounds, perm, q, offs, starts, k, vt, *refs):
     if last:
         perm_t, before, out, sorted_q, sorted_o, acc = refs
@@ -338,7 +338,7 @@
     key_span = pack_key_cache.shape[0]
     capacity = 2 * row_count // servers
     slot_count = servers * capacity
-    depth, head_width = w_query.shape
+    _, head_width = w_query.shape
     heads = head_width // HEAD_SIZE
 
     server = query_pos // key_span
@@ -355,12 +355,10 @@
     z = lax.axis_index("tensor") % N_Z
     far = far_hidden(hidden_rows, h, z)
     query_pieces = with_other_core(y_pieces(w_query, 0))
-    far_queries = far_product(far, query_pieces, jnp.stack([(y + N_Z - z) % N_Y, core]))
+    far_place = jnp.stack([(y + N_Z - z) % N_Y, core, h])
+    far_queries = part_product(far, query_pieces, far_place)
     hidden_rows, far_queries = lax.optimization_barrier((hidden_rows, far_queries))
-    queries = jnp.zeros((row_count, head_width), jnp.float32)
-    for piece, shift, first in query_pieces:
-        left = lax.dynamic_slice_in_dim(hidden_rows, member(me, shift) * depth + first, piece.shape[0], 1)
-        queries = queries + jnp.dot(left, piece, preferred_element_type=jnp.float32)
+    queries = part_product([], query_pieces, jnp.stack([y, core, h]), whole=hidden_rows)
     queries = rounded(queries + over_row(far_queries, H_FLIP))
     outgoing = rounded(jnp.dot(pack, queries, preferred_element_type=jnp.float32))
     slot_offset, pack_value_cache, outgoing = lax.optimization_barrier((slot_offset, pack_value_cache, outgoing))
@@ -382,7 +380,8 @@
     first = project(rows_of(unpack[:half]), out_pieces, place, groups, False)
     first = reduce_z(first)
     first = rounded(added(first[0], over_tensor(rounded(first[1]), XL_FLIP)))
-    second = rounded(reduce_z(rounded(added(mine, other))[:, None])[0])
+    second = rounded(added(mine, other))
+    second = rounded(reduce_z(second[:, None])[0])
     return jnp.concatenate([first, second], axis=0)
 
 

time: 288 us -> 291 us (1.010)
  waiting for transfers between devices: 98 us -> 116 us
  matrix products: 19.2 us -> 4.68 us
  Pallas kernels: 51.2 us -> 57.8 us
  starting transfers between devices: 80.5 us -> 75.4 us
    all_to_all x3, waiting for transfers between devices: 3.08 us -> 31.3 us  [exchange(): return lax.all_to_all(x, 'row', split_axis=0, concat_axis=0, tiled=True)]
    dot_general x9 -> x0, matrix products: 14.2 us -> none  [sublayer(): queries = queries + jnp.dot(left, piece, preferred_element_type=jnp.float32)]
    ppermute x18, waiting for transfers between devices: 43.4 us -> 35 us  [over_tensor(): return lax.ppermute(x, 'tensor', moves)]
    pallas_call x1 -> x2, Pallas kernels: 6.46 us -> 13 us  [part_product(): pl.pallas_call(functools.partial(part_kernel, [p[1:] for p in lefts], [p[...]
    ppermute x29, starting transfers between devices: 40.9 us -> 36.3 us  [over_row(): return lax.ppermute(x, 'row', moves)]
  transfers between devices with their start and end apart: 51 -> 51, of which waited for: 22 -> 22; matrix products, arithmetic and copies ran while one was open for 16% -> 11% of each run, Pallas kernels for 15% -> 17%
where the time goes in v1:
time: 291 us; the launch traced here: 287 us
  waiting for transfers between devices  116 us (40%)
  starting transfers between devices  75.4 us (26%)
  Pallas kernels  57.8 us (20%)
  local copies, waits for them, and re-layouts  23.2 us (8%)
  other arithmetic  6.67 us (2%)
  matrix products  4.68 us (2%)
    ppermute x29, waiting for transfers between devices, over_row(): return lax.ppermute(x, 'row', moves)  40.3 us
    ppermute x29, starting transfers between devices, over_row(): return lax.ppermute(x, 'row', moves)  36.3 us
    ppermute x18, waiting for transfers between devices, over_tensor(): return lax.ppermute(x, 'tensor', moves)  35 us
    all_to_all x3, waiting for transfers between devices, exchange(): return lax.all_to_all(x, 'row', split_axis=0, concat_axis=0, tiled=True)  31.3 us
    pallas_call x2, Pallas kernels, attend_run(): pl.pallas_call(functools.partial(attend_kernel, heads, first_tile, last),...  26.8 us
    all_to_all x3, starting transfers between devices, exchange(): return lax.all_to_all(x, 'row', split_axis=0, concat_axis=0, tiled=True)  19.1 us
    pallas_call x2, Pallas kernels, project(): pl.pallas_call(functools.partial(project_kernel, blocks, apart), out_shap...  18 us
    ppermute x18, starting transfers between devices, over_tensor(): return lax.ppermute(x, 'tensor', moves)  17.5 us
  transfers between devices with their start and end apart: 51, of which 22 were waited for; matrix products, arithmetic and copies ran while one was open for 11% of the time, Pallas kernels for 17%

profile of v1, /device:TPU:1, one launch (start us, length us, event | category | flops | bytes accessed | tf_op | source)
XLA Modules:
  0.0 287.0 jit_solution(15073086623533171062)
XLA Ops:
  8.6 9.7 %collective-permute-done.refs_0_ = bf16[256,1024]{1,0:T(8,128)(2,1)S(1)} collective-permute-done((bf16[256,1024]{1,0:T(8,128)(2,1)S(1)}, bf16[256,1024]{1,0:T(8,128)(2,1)S(1)}, u32[]{:S(2)}, u32[]{:S(2)}) %collective-permute-start) | collective-permute-done | bytes 524320 | tf_op jit(solution)/shard_map/ppermute | solution.py:71
  18.3 3.6 %collective-permute-start.1 = (bf16[256,1024]{1,0:T(8,128)(2,1)S(1)}, bf16[256,1024]{1,0:T(8,128)(2,1)S(1)}, u32[]{:S(2)}, u32[]{:S(2)}) collective-permute-start(bf16[256,1024]{1,0:T(8,128)(2,1)S(1)} %collective-permute-done.refs_0_), channel_id=1, source_target_pairs={{0,3},{1,0},{2,1},{3,2},{4,7},{5,4},{6,5},{7,6},{8,11},{9,8},{10,9... | collective-permute-start | bytes 1572872 | tf_op jit(solution)/shard_map/ppermute | solution.py:47
  22.0 4.5 %collective-permute-done.6.refs_7_.refs_3_ = bf16[512,1024]{1,0:T(8,128)(2,1)S(1)} collective-permute-done((bf16[512,1024]{1,0:T(8,128)(2,1)}, bf16[512,1024]{1,0:T(8,128)(2,1)S(1)}, u32[]{:S(2)}, u32[]{:S(2)}) %collective-permute-start.6) | collective-permute-done | bytes 1048608 | tf_op jit(solution)/shard_map/ppermute | solution.py:43
  28.1 3.2 %collective-permute-done.1.refs_1_ = bf16[256,1024]{1,0:T(8,128)(2,1)S(1)} collective-permute-done((bf16[256,1024]{1,0:T(8,128)(2,1)S(1)}, bf16[256,1024]{1,0:T(8,128)(2,1)S(1)}, u32[]{:S(2)}, u32[]{:S(2)}) %collective-permute-start.1) | collective-permute-done | bytes 524320 | tf_op jit(solution)/shard_map/ppermute | solution.py:47
  35.8 7.3 %collective-permute-done.10.refs_11_.refs_7_ = bf16[256,1024]{1,0:T(8,128)(2,1)} collective-permute-done((bf16[256,1024]{1,0:T(8,128)(2,1)S(1)}, bf16[256,1024]{1,0:T(8,128)(2,1)}, u32[]{:S(2)}, u32[]{:S(2)}) %collective-permute-start.10) | collective-permute-done | bytes 524320 | tf_op jit(solution)/shard_map/ppermute | solution.py:43
  43.2 3.7 %collective-permute-start.11 = (bf16[256,1024]{1,0:T(8,128)(2,1)}, bf16[256,1024]{1,0:T(8,128)(2,1)}, u32[]{:S(2)}, u32[]{:S(2)}) collective-permute-start(bf16[256,1024]{1,0:T(8,128)(2,1)} %collective-permute-done.10.refs_11_.refs_7_), channel_id=1, source_target_pairs={{0,8},{8,0},{16,24},{24,16},{32,40},{40,32},{48,56},{56,48},{64,72... | collective-permute-start | bytes 1572872 | tf_op jit(solution)/shard_map/ppermute | solution.py:43
  51.7 6.1 %collective-permute-done.4.refs_4_ = bf16[128,1024]{1,0:T(8,128)(2,1)} collective-permute-done((bf16[128,1024]{1,0:T(8,128)(2,1)}, bf16[128,1024]{1,0:T(8,128)(2,1)}, u32[]{:S(2)}, u32[]{:S(2)}) %collective-permute-start.4) | collective-permute-done | bytes 262176 | tf_op jit(solution)/shard_map/ppermute | solution.py:47
  62.9 6.5 %shard_map.73 = f32[256,1024]{1,0:T(8,128)} custom-call(s32[3]{0:T(128)} %add_add_fusion.1.place, bf16[256,1024]{1,0:T(8,128)(2,1)} %copy-done.11, bf16[256,1024]{1,0:T(8,128)(2,1)} %copy-done.8, bf16[256,1024]{1,0:T(8,128)(2,1)} %copy-done.9, bf16[128,1024]{1,0:T(8,128)(2,1)} %copy-done.12, bf16[128,1024]{1,0:T(8,128)(2,1)} %collective-permute-done.4.refs_4_, ...), custom_call_target="tpu_custom_call" | custom-call | tf_op jit(solution)/shard_map/pallas_call | solution.py:121
  72.0 5.3 %all-to-all-start = ((s32[16,1,32]{2,1,0:T(1,128)}), s32[16,1,32]{2,1,0:T(1,128)S(1)}, u32[]{:S(2)}, u32[]{:S(2)}) async-start(s32[16,1,32]{2,1,0:T(1,128)} %sub.40), calls=%async_computation | async-start | bytes 16384 | tf_op jit(solution)/shard_map/all_to_all | solution.py:308
  81.1 30.5 %all-to-all-done = s32[16,1,32]{2,1,0:T(1,128)S(1)} async-done(((s32[16,1,32]{2,1,0:T(1,128)}), s32[16,1,32]{2,1,0:T(1,128)S(1)}, u32[]{:S(2)}, u32[]{:S(2)}) %all-to-all-start) | async-done | bytes 2080 | tf_op jit(solution)/shard_map/all_to_all | solution.py:308
  117.3 6.5 %shard_map.74 = f32[256,1024]{1,0:T(8,128)} custom-call(s32[3]{0:T(128)} %add_add_fusion.place, bf16[256,8192]{1,0:T(8,128)(2,1)} %refs_0_.2, bf16[512,1024]{1,0:T(8,128)(2,1)} %refs_1_.1, bf16[512,1024]{1,0:T(8,128)(2,1)} %copy-done.7, bf16[512,1024]{1,0:T(8,128)(2,1)} %copy-done.3, bf16[512,1024]{1,0:T(8,128)(2,1)} %collective-permute-done.7.refs_8_.refs_4_, ...), custom_call_target="tpu_custom_call" | custom-call | tf_op jit(solution)/shard_map/pallas_call | solution.py:121
  130.9 5.3 %all-to-all-start.1 = ((bf16[16,32,1024]{2,1,0:T(8,128)(2,1)}), bf16[16,32,1024]{2,1,0:T(8,128)(2,1)S(1)}, u32[]{:S(2)}, u32[]{:S(2)}) async-start(bf16[16,32,1024]{2,1,0:T(8,128)(2,1)} %bitcast.66), calls=%async_computation.1 | async-start | bytes 2097152 | tf_op jit(solution)/shard_map/all_to_all | solution.py:308
  141.7 3.9 %copy.10 = bf16[8,1024,128]{1,2,0:T(8,128)(2,1)} copy(bf16[8,1024,128]{2,1,0:T(8,128)(2,1)} %bitcast.68) | data formatting | bytes 4194304 | tf_op jit(solution)/shard_map/reshape | solution.py:367
  147.6 8.5 %collective-permute-done.26.refs_12_ = bf16[1024,512]{1,0:T(8,128)(2,1)} collective-permute-done((bf16[1024,512]{1,0:T(8,128)(2,1)}, bf16[1024,512]{1,0:T(8,128)(2,1)}, u32[]{:S(2)}, u32[]{:S(2)}) %collective-permute-start.26) | collective-permute-done | bytes 1048608 | tf_op jit(solution)/shard_map/ppermute | solution.py:43
  156.1 3.4 %collective-permute-start.22 = (bf16[512,512]{1,0:T(8,128)(2,1)}, bf16[512,512]{1,0:T(8,128)(2,1)}, u32[]{:S(2)}, u32[]{:S(2)}) collective-permute-start(bf16[512,512]{1,0:T(8,128)(2,1)} %collective-permute-done.20.refs_6_), channel_id=1, source_target_pairs={{0,8},{8,0},{16,24},{24,16},{32,40},{40,32},{48,56},{56,48},{64,72... | collective-permute-start | bytes 1572872 | tf_op jit(solution)/shard_map/ppermute | solution.py:43
  163.8 21.7 %shard_map.75.refs_1_ = bf16[320,1024]{1,0:T(8,128)(2,1)} custom-call(s32[2,8]{1,0:T(2,128)} %pad_add_fusion.bounds, bf16[320,512]{1,0:T(8,128)(2,1)} %slice.249.perm, bf16[512,1024]{1,0:T(8,128)(2,1)} %bitcast.64, s32[5,1,512]{2,1,0:T(1,128)} %slice.210.offs, s32[5,1,512]{2,1,0:T(1,128)} %slice.213.starts, bf16[8192,128]{1,0:T(8,128)(2,1)} %k.3, ...), custom_call_target="tpu_custom_call" | custom-call | tf_op jit(solution)/shard_map/pallas_call | solution.py:291
  185.5 5.1 %shard_map.76 = bf16[512,1024]{1,0:T(8,128)(2,1)} custom-call(s32[2,8]{1,0:T(2,128)} %pad_add_fusion.bounds, bf16[192,512]{1,0:T(8,128)(2,1)} %slice.248.perm, bf16[512,1024]{1,0:T(8,128)(2,1)} %bitcast.65, s32[3,1,512]{2,1,0:T(1,128)} %slice.203.offs, s32[3,1,512]{2,1,0:T(1,128)} %slice.206.starts, bf16[8192,128]{1,0:T(8,128)(2,1)} %k.3, ...), custom_call_target="tpu_custom_call" | custom-call | tf_op jit(solution)/shard_map/pallas_call | solution.py:291
  190.6 8.5 %all-to-all-start.2 = ((bf16[16,32,1024]{2,1,0:T(8,128)(2,1)}), bf16[16,32,1024]{2,1,0:T(8,128)(2,1)S(1)}, u32[]{:S(2)}, u32[]{:S(2)}) async-start(bf16[16,32,1024]{2,1,0:T(8,128)(2,1)} %bitcast.67), calls=%async_computation.2 | async-start | bytes 2097152 | tf_op jit(solution)/shard_map/all_to_all | solution.py:308
  205.2 19.9 %collective-permute-done.30.refs_16_ = bf16[512,512]{1,0:T(8,128)(2,1)} collective-permute-done((bf16[512,512]{1,0:T(8,128)(2,1)S(1)}, bf16[512,512]{1,0:T(8,128)(2,1)}, u32[]{:S(2)}, u32[]{:S(2)}) %collective-permute-start.30) | collective-permute-done | bytes 524320 | tf_op jit(solution)/shard_map/ppermute | solution.py:43
  230.3 9.0 %shard_map.78 = (bf16[4,128,1024]{2,1,0:T(8,128)(2,1)}, bf16[4,128,1024]{2,1,0:T(8,128)(2,1)}) custom-call(s32[5]{0:T(128)} %stack.42.place, bf16[128,1024]{1,0:T(8,128)(2,1)} %convolution_convert_fusion.1.rows, bf16[1024,512]{1,0:T(8,128)(2,1)} %refs_0_.4, bf16[1024,512]{1,0:T(8,128)(2,1)} %collective-permute-done.15.refs_1_, bf16[1024,512]{1,0:T(8,128)(2,1)} %copy-done.1, ...), custom_call_target="tpu_custom_call" | custom-call | tf_op jit(solution)/shard_map/pallas_call | solution.py:176
  240.9 8.9 %shard_map.77 = bf16[4,2,128,1024]{3,2,1,0:T(8,128)(2,1)} custom-call(s32[5]{0:T(128)} %stack.42.place, bf16[128,1024]{1,0:T(8,128)(2,1)} %convolution_convert_fusion.2.rows, bf16[1024,512]{1,0:T(8,128)(2,1)} %refs_0_.4, bf16[1024,512]{1,0:T(8,128)(2,1)} %collective-permute-done.15.refs_1_, bf16[1024,512]{1,0:T(8,128)(2,1)} %copy-done.1, ...), custom_call_target="tpu_custom_call" | custom-call | tf_op jit(solution)/shard_map/pallas_call | solution.py:176
  259.5 3.5 %collective-permute-start.39 = (bf16[2,64,1024]{2,1,0:T(8,128)(2,1)S(1)}, bf16[2,64,1024]{2,1,0:T(8,128)(2,1)S(1)}, u32[]{:S(2)}, u32[]{:S(2)}) collective-permute-start(bf16[2,64,1024]{2,1,0:T(8,128)(2,1)S(1)} %add_convert_fusion.3), channel_id=1, source_target_pairs={{0,3},{1,0},{2,1},{3,2},{4,7},{5,4},{6,5},{7,6},{8,11},{9,8},{10,9... | collective-permute-start | bytes 786440 | tf_op jit(solution)/shard_map/ppermute | solution.py:47
  264.5 3.7 %collective-permute-done.37 = bf16[2,64,1024]{2,1,0:T(8,128)(2,1)S(1)} collective-permute-done((bf16[2,64,1024]{2,1,0:T(8,128)(2,1)S(1)}, bf16[2,64,1024]{2,1,0:T(8,128)(2,1)S(1)}, u32[]{:S(2)}, u32[]{:S(2)}) %collective-permute-start.37) | collective-permute-done | bytes 262176 | tf_op jit(solution)/shard_map/ppermute | solution.py:47
  270.7 3.1 %collective-permute-done.36 = bf16[2,64,1024]{2,1,0:T(8,128)(2,1)S(1)} collective-permute-done((bf16[2,64,1024]{2,1,0:T(8,128)(2,1)S(1)}, bf16[2,64,1024]{2,1,0:T(8,128)(2,1)S(1)}, u32[]{:S(2)}, u32[]{:S(2)}) %collective-permute-start.36) | collective-permute-done | bytes 262176 | tf_op jit(solution)/shard_map/ppermute | solution.py:47
  (183 shorter events, 92.5 us)
Async XLA Ops:
  0.0 26.5 %collective-permute-start.6 = (bf16[512,1024]{1,0:T(8,128)(2,1)}, bf16[512,1024]{1,0:T(8,128)(2,1)S(1)}, u32[]{:S(2)}, u32[]{:S(2)}) collective-permute-start(bf16[512,1024]{1,0:T(8,128)(2,1)} %refs_1_.1), channel_id=1, source_target_pairs={{0,32},{8,40},{16,48},{24,56},{32,64},{40,72},{48,80},{56,88},{64,... | collective-permute-start | bytes 3145736 | tf_op jit(solution)/shard_map/ppermute | solution.py:43
  2.1 25.8 %collective-permute-start.8 = (bf16[512,1024]{1,0:T(8,128)(2,1)}, bf16[512,1024]{1,0:T(8,128)(2,1)S(1)}, u32[]{:S(2)}, u32[]{:S(2)}) collective-permute-start(bf16[512,1024]{1,0:T(8,128)(2,1)} %refs_1_.1), channel_id=1, source_target_pairs={{0,96},{8,104},{16,112},{24,120},{32,0},{40,8},{48,16},{56,24},{64... | collective-permute-start | bytes 3145736 | tf_op jit(solution)/shard_map/ppermute | solution.py:43
  7.2 28.5 %collective-permute-start.5 = (bf16[512,1024]{1,0:T(8,128)(2,1)}, bf16[512,1024]{1,0:T(8,128)(2,1)S(1)}, u32[]{:S(2)}, u32[]{:S(2)}) collective-permute-start(bf16[512,1024]{1,0:T(8,128)(2,1)} %refs_1_.1), channel_id=1, source_target_pairs={{0,8},{8,0},{16,24},{24,16},{32,40},{40,32},{48,56},{56,48},{64,72... | collective-permute-start | bytes 3145736 | tf_op jit(solution)/shard_map/ppermute | solution.py:43
  26.5 32.2 %collective-permute-start.7 = (bf16[512,1024]{1,0:T(8,128)(2,1)S(1)}, bf16[512,1024]{1,0:T(8,128)(2,1)}, u32[]{:S(2)}, u32[]{:S(2)}) collective-permute-start(bf16[512,1024]{1,0:T(8,128)(2,1)S(1)} %collective-permute-done.6.refs_7_.refs_3_), channel_id=1, source_target_pairs={{0,8},{8,0},{16,24},{24,16},{32,40},{40,32},{48,56},{56,48},{64,72... | collective-permute-start | bytes 3145736 | tf_op jit(solution)/shard_map/ppermute | solution.py:43
  27.9 30.8 %collective-permute-start.9 = (bf16[512,1024]{1,0:T(8,128)(2,1)S(1)}, bf16[512,1024]{1,0:T(8,128)(2,1)}, u32[]{:S(2)}, u32[]{:S(2)}) collective-permute-start(bf16[512,1024]{1,0:T(8,128)(2,1)S(1)} %collective-permute-done.8.refs_9_.refs_5_), channel_id=1, source_target_pairs={{0,8},{8,0},{16,24},{24,16},{32,40},{40,32},{48,56},{56,48},{64,72... | collective-permute-start | bytes 3145736 | tf_op jit(solution)/shard_map/ppermute | solution.py:43
  57.8 143.4 %collective-permute-start.15 = (bf16[1024,512]{1,0:T(8,128)(2,1)}, bf16[1024,512]{1,0:T(8,128)(2,1)}, u32[]{:S(2)}, u32[]{:S(2)}) collective-permute-start(bf16[1024,512]{1,0:T(8,128)(2,1)} %refs_0_.4), channel_id=1, source_target_pairs={{0,8},{8,0},{16,24},{24,16},{32,40},{40,32},{48,56},{56,48},{64,72... | collective-permute-start | bytes 3145736 | tf_op jit(solution)/shard_map/ppermute | solution.py:43
  58.7 54.1 %collective-permute-start.16 = (bf16[1024,512]{1,0:T(8,128)(2,1)}, bf16[1024,512]{1,0:T(8,128)(2,1)S(1)}, u32[]{:S(2)}, u32[]{:S(2)}) collective-permute-start(bf16[1024,512]{1,0:T(8,128)(2,1)} %refs_0_.4), channel_id=1, source_target_pairs={{0,32},{8,40},{16,48},{24,56},{32,64},{40,72},{48,80},{56,88},{64,... | collective-permute-start | bytes 3145736 | tf_op jit(solution)/shard_map/ppermute | solution.py:43
  58.7 55.6 %collective-permute-start.18 = (bf16[1024,512]{1,0:T(8,128)(2,1)}, bf16[1024,512]{1,0:T(8,128)(2,1)S(1)}, u32[]{:S(2)}, u32[]{:S(2)}) collective-permute-start(bf16[1024,512]{1,0:T(8,128)(2,1)} %refs_0_.4), channel_id=1, source_target_pairs={{0,96},{8,104},{16,112},{24,120},{32,0},{40,8},{48,16},{56,24},{64... | collective-permute-start | bytes 3145736 | tf_op jit(solution)/shard_map/ppermute | solution.py:43
  61.4 55.9 %collective-permute-start.24 = (bf16[1024,512]{1,0:T(8,128)(2,1)}, bf16[1024,512]{1,0:T(8,128)(2,1)}, u32[]{:S(2)}, u32[]{:S(2)}) collective-permute-start(bf16[1024,512]{1,0:T(8,128)(2,1)} %refs_0_.4), channel_id=1, source_target_pairs={{0,16},{8,24},{16,0},{24,8},{32,48},{40,56},{48,32},{56,40},{64,80... | collective-permute-start | bytes 3145736 | tf_op jit(solution)/shard_map/ppermute | solution.py:43
  69.4 54.4 %collective-permute-start.14 = (f32[256,1024]{1,0:T(8,128)}, f32[256,1024]{1,0:T(8,128)S(1)}, u32[]{:S(2)}, u32[]{:S(2)}) collective-permute-start(f32[256,1024]{1,0:T(8,128)} %shard_map.73), channel_id=1, source_target_pairs={{0,16},{8,24},{16,0},{24,8},{32,48},{40,56},{48,32},{56,40},{64,80... | collective-permute-start | bytes 3145736 | tf_op jit(solution)/shard_map/ppermute | solution.py:43
  72.0 39.6 %all-to-all-start = ((s32[16,1,32]{2,1,0:T(1,128)}), s32[16,1,32]{2,1,0:T(1,128)S(1)}, u32[]{:S(2)}, u32[]{:S(2)}) async-start(s32[16,1,32]{2,1,0:T(1,128)} %sub.40), calls=%async_computation | async-start | bytes 16384 | tf_op jit(solution)/shard_map/all_to_all | solution.py:308
  113.7 26.9 %collective-permute-start.20 = (bf16[512,512]{1,0:T(8,128)(2,1)}, bf16[512,512]{1,0:T(8,128)(2,1)}, u32[]{:S(2)}, u32[]{:S(2)}) collective-permute-start(bf16[512,512]{1,0:T(8,128)(2,1)} %slice.250), channel_id=1, source_target_pairs={{0,32},{8,40},{16,48},{24,56},{32,64},{40,72},{48,80},{56,88},{64,... | collective-permute-start | bytes 1572872 | tf_op jit(solution)/shard_map/ppermute | solution.py:43
  115.2 31.9 %collective-permute-start.21 = (bf16[512,512]{1,0:T(8,128)(2,1)}, bf16[512,512]{1,0:T(8,128)(2,1)}, u32[]{:S(2)}, u32[]{:S(2)}) collective-permute-start(bf16[512,512]{1,0:T(8,128)(2,1)} %slice.251), channel_id=1, source_target_pairs={{0,96},{8,104},{16,112},{24,120},{32,0},{40,8},{48,16},{56,24},{64... | collective-permute-start | bytes 1572872 | tf_op jit(solution)/shard_map/ppermute | solution.py:43
  117.3 38.8 %collective-permute-start.26 = (bf16[1024,512]{1,0:T(8,128)(2,1)}, bf16[1024,512]{1,0:T(8,128)(2,1)}, u32[]{:S(2)}, u32[]{:S(2)}) collective-permute-start(bf16[1024,512]{1,0:T(8,128)(2,1)} %collective-permute-done.24.refs_10_), channel_id=1, source_target_pairs={{0,32},{8,40},{16,48},{24,56},{32,64},{40,72},{48,80},{56,88},{64,... | collective-permute-start | bytes 3145736 | tf_op jit(solution)/shard_map/ppermute | solution.py:43
  123.8 35.7 %collective-permute-start.28 = (bf16[1024,512]{1,0:T(8,128)(2,1)}, bf16[1024,512]{1,0:T(8,128)(2,1)}, u32[]{:S(2)}, u32[]{:S(2)}) collective-permute-start(bf16[1024,512]{1,0:T(8,128)(2,1)} %collective-permute-done.24.refs_10_), channel_id=1, source_target_pairs={{0,96},{8,104},{16,112},{24,120},{32,0},{40,8},{48,16},{56,24},{64... | collective-permute-start | bytes 3145736 | tf_op jit(solution)/shard_map/ppermute | solution.py:43
  130.9 31.9 %all-to-all-start.1 = ((bf16[16,32,1024]{2,1,0:T(8,128)(2,1)}), bf16[16,32,1024]{2,1,0:T(8,128)(2,1)S(1)}, u32[]{:S(2)}, u32[]{:S(2)}) async-start(bf16[16,32,1024]{2,1,0:T(8,128)(2,1)} %bitcast.66), calls=%async_computation.1 | async-start | bytes 2097152 | tf_op jit(solution)/shard_map/all_to_all | solution.py:308
  140.6 62.1 %collective-permute-start.17 = (bf16[1024,512]{1,0:T(8,128)(2,1)S(1)}, bf16[1024,512]{1,0:T(8,128)(2,1)}, u32[]{:S(2)}, u32[]{:S(2)}) collective-permute-start(bf16[1024,512]{1,0:T(8,128)(2,1)S(1)} %collective-permute-done.16.refs_2_), channel_id=1, source_target_pairs={{0,8},{8,0},{16,24},{24,16},{32,40},{40,32},{48,56},{56,48},{64,72... | collective-permute-start | bytes 3145736 | tf_op jit(solution)/shard_map/ppermute | solution.py:43
  147.1 56.9 %collective-permute-start.19 = (bf16[1024,512]{1,0:T(8,128)(2,1)S(1)}, bf16[1024,512]{1,0:T(8,128)(2,1)}, u32[]{:S(2)}, u32[]{:S(2)}) collective-permute-start(bf16[1024,512]{1,0:T(8,128)(2,1)S(1)} %collective-permute-done.18.refs_4_), channel_id=1, source_target_pairs={{0,8},{8,0},{16,24},{24,16},{32,40},{40,32},{48,56},{56,48},{64,72... | collective-permute-start | bytes 3145736 | tf_op jit(solution)/shard_map/ppermute | solution.py:43
  156.1 48.6 %collective-permute-start.22 = (bf16[512,512]{1,0:T(8,128)(2,1)}, bf16[512,512]{1,0:T(8,128)(2,1)}, u32[]{:S(2)}, u32[]{:S(2)}) collective-permute-start(bf16[512,512]{1,0:T(8,128)(2,1)} %collective-permute-done.20.refs_6_), channel_id=1, source_target_pairs={{0,8},{8,0},{16,24},{24,16},{32,40},{40,32},{48,56},{56,48},{64,72... | collective-permute-start | bytes 1572872 | tf_op jit(solution)/shard_map/ppermute | solution.py:43
  159.5 45.2 %collective-permute-start.23 = (bf16[512,512]{1,0:T(8,128)(2,1)}, bf16[512,512]{1,0:T(8,128)(2,1)}, u32[]{:S(2)}, u32[]{:S(2)}) collective-permute-start(bf16[512,512]{1,0:T(8,128)(2,1)} %collective-permute-done.21.refs_7_), channel_id=1, source_target_pairs={{0,8},{8,0},{16,24},{24,16},{32,40},{40,32},{48,56},{56,48},{64,72... | collective-permute-start | bytes 1572872 | tf_op jit(solution)/shard_map/ppermute | solution.py:43
  190.6 36.3 %all-to-all-start.2 = ((bf16[16,32,1024]{2,1,0:T(8,128)(2,1)}), bf16[16,32,1024]{2,1,0:T(8,128)(2,1)S(1)}, u32[]{:S(2)}, u32[]{:S(2)}) async-start(bf16[16,32,1024]{2,1,0:T(8,128)(2,1)} %bitcast.67), calls=%async_computation.2 | async-start | bytes 2097152 | tf_op jit(solution)/shard_map/all_to_all | solution.py:308
  204.0 24.9 %collective-permute-start.25 = (bf16[1024,512]{1,0:T(8,128)(2,1)}, bf16[1024,512]{1,0:T(8,128)(2,1)S(1)}, u32[]{:S(2)}, u32[]{:S(2)}) collective-permute-start(bf16[1024,512]{1,0:T(8,128)(2,1)} %collective-permute-done.24.refs_10_), channel_id=1, source_target_pairs={{0,8},{8,0},{16,24},{24,16},{32,40},{40,32},{48,56},{56,48},{64,72... | collective-permute-start | bytes 3145736 | tf_op jit(solution)/shard_map/ppermute | solution.py:43
  204.7 24.3 %collective-permute-start.27 = (bf16[1024,512]{1,0:T(8,128)(2,1)}, bf16[1024,512]{1,0:T(8,128)(2,1)S(1)}, u32[]{:S(2)}, u32[]{:S(2)}) collective-permute-start(bf16[1024,512]{1,0:T(8,128)(2,1)} %collective-permute-done.26.refs_12_), channel_id=1, source_target_pairs={{0,8},{8,0},{16,24},{24,16},{32,40},{40,32},{48,56},{56,48},{64,72... | collective-permute-start | bytes 3145736 | tf_op jit(solution)/shard_map/ppermute | solution.py:43
  239.3 24.6 %collective-permute-start.41 = (bf16[4,128,1024]{2,1,0:T(8,128)(2,1)}, bf16[4,128,1024]{2,1,0:T(8,128)(2,1)S(1)}, u32[]{:S(2)}, u32[]{:S(2)}) collective-permute-start(bf16[4,128,1024]{2,1,0:T(8,128)(2,1)} %get-tuple-element.18), channel_id=1, source_target_pairs={{0,4},{1,5},{2,6},{3,7},{4,0},{5,1},{6,2},{7,3},{8,12},{9,13},{10,... | collective-permute-start | bytes 3145736 | tf_op jit(solution)/shard_map/ppermute | solution.py:47
  (42 other events, 594.4 us)

commit v2 on v1

--- a/solution.py
+++ b/solution.py
@@ -132,18 +132,15 @@
     )(place, *left_arrays, *right_arrays)
 
 
-def project_kernel(blocks, apart, place, rows, *refs):
+def project_kernel(blocks, place, rows, *refs):
     count = sum(len(parts) for _, parts in blocks)
-    pieces, refs = refs[:count], refs[count:]
-    if apart:
-        mine, other, total_buf, refs = refs[0], refs[1], refs[-2], refs[2:-2] + refs[-1:]
-    else:
-        total_buf, refs = refs[0], refs[1:]
-    bufs, sems = refs[:-1], refs[-1]
+    pieces, (first_rows, mine, other), bufs, second_rows, sems = (
+        refs[:count], refs[count:count + 3], refs[count + 3:-2], refs[-2], refs[-1]
+    )
     copies = [pltpu.make_async_copy(pieces[i], bufs[i], sems.at[i]) for i in range(count)]
     for copy in copies:
         copy.start()
-    width = pieces[0].shape[1]
+    width, half = pieces[0].shape[1], rows.shape[0] // 2
     i = 0
     for (dy, dh, dc), firsts in blocks:
         total = None
@@ -153,34 +150,35 @@
             term = jnp.dot(rows[:, first:first + depth], bufs[i][...], preferred_element_type=jnp.float32)
             total = term if total is None else total + term
             i += 1
+        total = total.astype(jnp.bfloat16)
         group = lax.rem(place[0] + dy, N_Y) * N_XH + lax.rem(place[1] + dh, N_XH)
         to_xl = lax.rem(group // N_Z + place[3], N_XL)
         to_z = lax.rem(lax.rem(group, N_Z) + N_Z - place[4], N_Z)
         begin = pl.multiple_of(lax.rem(place[2] + dc, N_CORE) * width, width)
-        total_buf[to_z, to_xl, :, pl.ds(begin, width)] = total.astype(jnp.bfloat16)
-    if apart:
-        mine[...] = total_buf[:, 0]
-        other[...] = total_buf[:, 1]
-
-
-def project(rows, pieces, place, groups, apart):
+        first_rows[to_z, to_xl, :, pl.ds(begin, width)] = total[:half]
+        second_rows[to_z, to_xl, :, pl.ds(begin, width)] = total[half:]
+    mine[...] = second_rows[:, 0]
+    other[...] = second_rows[:, 1]
+
+
+def project(rows, pieces, place, groups):
     by_block = {}
     for piece, shift, first in pieces:
         by_block.setdefault(shift, []).append((first, piece))
     blocks = tuple((shift, tuple(first for first, _ in parts)) for shift, parts in by_block.items())
     arrays = [piece for parts in by_block.values() for _, piece in parts]
-    count, width = rows.shape[0], len(blocks) * arrays[0].shape[1] // groups
+    half, width = rows.shape[0] // 2, len(blocks) * arrays[0].shape[1] // groups
     vmem = pl.BlockSpec(memory_space=pltpu.VMEM)
-    whole = (N_Z, N_XL, count, width)
-    one = jax.ShapeDtypeStruct((N_Z, count, width), jnp.bfloat16)
+    both = (N_Z, N_XL, half, width)
+    one = jax.ShapeDtypeStruct((N_Z, half, width), jnp.bfloat16)
     return pl.pallas_call(
-        functools.partial(project_kernel, blocks, apart),
-        out_shape=(one, one) if apart else jax.ShapeDtypeStruct(whole, jnp.bfloat16),
+        functools.partial(project_kernel, blocks),
+        out_shape=(jax.ShapeDtypeStruct(both, jnp.bfloat16), one, one),
         in_specs=[pl.BlockSpec(memory_space=pltpu.SMEM), vmem] + [pl.BlockSpec(memory_space=pl.ANY)] * len(arrays),
-        out_specs=(vmem, vmem) if apart else vmem,
+        out_specs=(vmem, vmem, vmem),
         scratch_shapes=[pltpu.VMEM(a.shape, a.dtype) for a in arrays]
-        + ([pltpu.VMEM(whole, jnp.bfloat16)] if apart else [])
-        + [pltpu.SemaphoreType.DMA((len(arrays),))],
+        + [pltpu.VMEM(both, jnp.bfloat16), pltpu.SemaphoreType.DMA((len(arrays),))],
+        name="project",
     )(place, rows, *arrays)
 
 
@@ -299,7 +297,7 @@
 
 def attend(q, tables, k, vt):
     tiles = q.shape[0] // TILE
-    cut = (tiles * 5 + 7) // 8
+    cut = (tiles + 1) // 2
     before = attend_run(q, tables, k, vt, None, 0, cut)
     return attend_run(q, tables, k, vt, before, cut, tiles)
 
@@ -371,13 +369,10 @@
 
     attended = attend(incoming, tables, pack_key_cache, vt)
     returned = exchange(attended.reshape(servers, capacity, head_width)).reshape(slot_count, head_width)
-    half = row_count // 2
-    rows_of = lambda part: rounded(jnp.dot(part, returned, preferred_element_type=jnp.float32))
-    t = lax.axis_index("tensor")
-    place = jnp.stack([y, h, core, t // N_Z, z])
-    mine, other = project(rows_of(unpack[half:]), out_pieces, place, groups, True)
+    own_rows = rounded(jnp.dot(unpack, returned, preferred_element_type=jnp.float32))
+    place = jnp.stack([y, h, core, lax.axis_index("tensor") // N_Z, z])
+    first, mine, other = project(own_rows, out_pieces, place, groups)
     other = over_tensor(other, XL_FLIP)
-    first = project(rows_of(unpack[:half]), out_pieces, place, groups, False)
     first = reduce_z(first)
     first = rounded(added(first[0], over_tensor(rounded(first[1]), XL_FLIP)))
     second = rounded(added(mine, other))

time: 291 us -> 281 us (0.966)
  starting transfers between devices: 75.4 us -> 85.7 us
  waiting for transfers between devices: 116 us -> 109 us
  Pallas kernels: 57.8 us -> 50.9 us
  local copies, waits for them, and re-layouts: 23.2 us -> 19.2 us
    pallas_call x2 -> x1, Pallas kernels: 18 us -> 11.6 us  [project(): pl.pallas_call(functools.partial(project_kernel, blocks), out_shape=(jax....]
    ppermute x18, starting transfers between devices: 17.5 us -> 22.9 us  [over_tensor(): return lax.ppermute(x, 'tensor', moves)]
    ppermute x18, waiting for transfers between devices: 35 us -> 30.4 us  [over_tensor(): return lax.ppermute(x, 'tensor', moves)]
    all_to_all x3, waiting for transfers between devices: 31.3 us -> 26.9 us  [exchange(): return lax.all_to_all(x, 'row', split_axis=0, concat_axis=0, tiled=True)]
    all_to_all x3, starting transfers between devices: 19.1 us -> 22.3 us  [exchange(): return lax.all_to_all(x, 'row', split_axis=0, concat_axis=0, tiled=True)]
  transfers between devices with their start and end apart: 51 -> 51, of which waited for: 22 -> 17; matrix products, arithmetic and copies ran while one was open for 11% -> 10% of each run, Pallas kernels for 17% -> 14%
where the time goes in v2:
time: 281 us; the launch traced here: 278 us
  waiting for transfers between devices  109 us (39%)
  starting transfers between devices  85.7 us (30%)
  Pallas kernels  50.9 us (18%)
  local copies, waits for them, and re-layouts  19.2 us (7%)
  other arithmetic  6.45 us (2%)
  matrix products  3.94 us (1%)
  between operations  2.93 us (1%)
    ppermute x29, waiting for transfers between devices, over_row(): return lax.ppermute(x, 'row', moves)  41.7 us
    ppermute x29, starting transfers between devices, over_row(): return lax.ppermute(x, 'row', moves)  37.8 us
    ppermute x18, waiting for transfers between devices, over_tensor(): return lax.ppermute(x, 'tensor', moves)  30.4 us
    all_to_all x3, waiting for transfers between devices, exchange(): return lax.all_to_all(x, 'row', split_axis=0, concat_axis=0, tiled=True)  26.9 us
    pallas_call x2, Pallas kernels, attend_run(): pl.pallas_call(functools.partial(attend_kernel, heads, first_tile, last),...  26.3 us
    ppermute x18, starting transfers between devices, over_tensor(): return lax.ppermute(x, 'tensor', moves)  22.9 us
    all_to_all x3, starting transfers between devices, exchange(): return lax.all_to_all(x, 'row', split_axis=0, concat_axis=0, tiled=True)  22.3 us
    pallas_call x2, Pallas kernels, part_product(): pl.pallas_call(functools.partial(part_kernel, [p[1:] for p in lefts], [p[...  13 us
  transfers between devices with their start and end apart: 51, of which 17 were waited for; matrix products, arithmetic and copies ran while one was open for 10% of the time, Pallas kernels for 14%

profile of v2, /device:TPU:1, one launch (start us, length us, event | category | flops | bytes accessed | tf_op | source)
XLA Modules:
  0.0 277.8 jit_solution(8273539541706117699)
XLA Ops:
  8.6 9.7 %collective-permute-done.refs_0_ = bf16[256,1024]{1,0:T(8,128)(2,1)S(1)} collective-permute-done((bf16[256,1024]{1,0:T(8,128)(2,1)S(1)}, bf16[256,1024]{1,0:T(8,128)(2,1)S(1)}, u32[]{:S(2)}, u32[]{:S(2)}) %collective-permute-start) | collective-permute-done | bytes 524320 | tf_op jit(solution)/shard_map/ppermute | solution.py:71
  22.0 4.5 %collective-permute-done.6.refs_7_.refs_3_ = bf16[512,1024]{1,0:T(8,128)(2,1)S(1)} collective-permute-done((bf16[512,1024]{1,0:T(8,128)(2,1)}, bf16[512,1024]{1,0:T(8,128)(2,1)S(1)}, u32[]{:S(2)}, u32[]{:S(2)}) %collective-permute-start.6) | collective-permute-done | bytes 1048608 | tf_op jit(solution)/shard_map/ppermute | solution.py:43
  29.4 2.9 %collective-permute-done.2.refs_2_ = bf16[256,1024]{1,0:T(8,128)(2,1)S(1)} collective-permute-done((bf16[256,1024]{1,0:T(8,128)(2,1)S(1)}, bf16[256,1024]{1,0:T(8,128)(2,1)S(1)}, u32[]{:S(2)}, u32[]{:S(2)}) %collective-permute-start.2) | collective-permute-done | bytes 524320 | tf_op jit(solution)/shard_map/ppermute | solution.py:47
  36.0 4.1 %collective-permute-done.10.refs_11_.refs_7_ = bf16[256,1024]{1,0:T(8,128)(2,1)} collective-permute-done((bf16[256,1024]{1,0:T(8,128)(2,1)S(1)}, bf16[256,1024]{1,0:T(8,128)(2,1)}, u32[]{:S(2)}, u32[]{:S(2)}) %collective-permute-start.10) | collective-permute-done | bytes 524320 | tf_op jit(solution)/shard_map/ppermute | solution.py:43
  43.6 3.2 %collective-permute-start.4 = (bf16[128,1024]{1,0:T(8,128)(2,1)}, bf16[128,1024]{1,0:T(8,128)(2,1)}, u32[]{:S(2)}, u32[]{:S(2)}) collective-permute-start(bf16[128,1024]{1,0:T(8,128)(2,1)} %slice.236), channel_id=1, source_target_pairs={{0,3},{1,0},{2,1},{3,2},{4,7},{5,4},{6,5},{7,6},{8,11},{9,8},{10,9... | collective-permute-start | bytes 786440 | tf_op jit(solution)/shard_map/ppermute | solution.py:47
  47.4 4.8 %collective-permute-done.4.refs_4_ = bf16[128,1024]{1,0:T(8,128)(2,1)} collective-permute-done((bf16[128,1024]{1,0:T(8,128)(2,1)}, bf16[128,1024]{1,0:T(8,128)(2,1)}, u32[]{:S(2)}, u32[]{:S(2)}) %collective-permute-start.4) | collective-permute-done | bytes 262176 | tf_op jit(solution)/shard_map/ppermute | solution.py:47
  59.9 6.5 %shard_map.73 = f32[256,1024]{1,0:T(8,128)} custom-call(s32[3]{0:T(128)} %add_add_fusion.1.place, bf16[256,1024]{1,0:T(8,128)(2,1)} %copy-done.9, bf16[256,1024]{1,0:T(8,128)(2,1)} %copy-done.7, bf16[256,1024]{1,0:T(8,128)(2,1)} %copy-done.6, bf16[128,1024]{1,0:T(8,128)(2,1)} %copy-done.10, bf16[128,1024]{1,0:T(8,128)(2,1)} %collective-permute-done.4.refs_4_, ...), custom_call_target="tpu_custom_call" | custom-call | tf_op jit(solution)/shard_map/pallas_call | solution.py:121
  67.7 5.9 %all-to-all-start = ((s32[16,1,32]{2,1,0:T(1,128)}), s32[16,1,32]{2,1,0:T(1,128)S(1)}, u32[]{:S(2)}, u32[]{:S(2)}) async-start(s32[16,1,32]{2,1,0:T(1,128)} %sub.40), calls=%async_computation | async-start | bytes 16384 | tf_op jit(solution)/shard_map/all_to_all | solution.py:306
  77.5 26.9 %all-to-all-done = s32[16,1,32]{2,1,0:T(1,128)S(1)} async-done(((s32[16,1,32]{2,1,0:T(1,128)}), s32[16,1,32]{2,1,0:T(1,128)S(1)}, u32[]{:S(2)}, u32[]{:S(2)}) %all-to-all-start) | async-done | bytes 2080 | tf_op jit(solution)/shard_map/all_to_all | solution.py:306
  112.1 6.5 %shard_map.74 = f32[256,1024]{1,0:T(8,128)} custom-call(s32[3]{0:T(128)} %add_add_fusion.place, bf16[256,8192]{1,0:T(8,128)(2,1)} %refs_0_.1, bf16[512,1024]{1,0:T(8,128)(2,1)} %refs_1_.1, bf16[512,1024]{1,0:T(8,128)(2,1)} %copy-done.3, bf16[512,1024]{1,0:T(8,128)(2,1)} %copy-done.1, bf16[512,1024]{1,0:T(8,128)(2,1)} %collective-permute-done.7.refs_8_.refs_4_, ...), custom_call_target="tpu_custom_call" | custom-call | tf_op jit(solution)/shard_map/pallas_call | solution.py:121
  118.6 2.9 %collective-permute-start.28 = (bf16[1024,512]{1,0:T(8,128)(2,1)}, bf16[1024,512]{1,0:T(8,128)(2,1)S(1)}, u32[]{:S(2)}, u32[]{:S(2)}) collective-permute-start(bf16[1024,512]{1,0:T(8,128)(2,1)} %collective-permute-done.24.refs_10_), channel_id=1, source_target_pairs={{0,96},{8,104},{16,112},{24,120},{32,0},{40,8},{48,16},{56,24},{64... | collective-permute-start | bytes 3145736 | tf_op jit(solution)/shard_map/ppermute | solution.py:43
  124.8 6.1 %all-to-all-start.1 = ((bf16[16,32,1024]{2,1,0:T(8,128)(2,1)}), bf16[16,32,1024]{2,1,0:T(8,128)(2,1)S(1)}, u32[]{:S(2)}, u32[]{:S(2)}) async-start(bf16[16,32,1024]{2,1,0:T(8,128)(2,1)} %bitcast.11), calls=%async_computation.1 | async-start | bytes 2097152 | tf_op jit(solution)/shard_map/all_to_all | solution.py:306
  131.8 3.9 %copy.10 = bf16[8,1024,128]{1,2,0:T(8,128)(2,1)} copy(bf16[8,1024,128]{2,1,0:T(8,128)(2,1)} %bitcast.63) | data formatting | bytes 4194304 | tf_op jit(solution)/shard_map/reshape | solution.py:365
  139.7 10.1 %collective-permute-done.26.refs_12_ = bf16[1024,512]{1,0:T(8,128)(2,1)S(1)} collective-permute-done((bf16[1024,512]{1,0:T(8,128)(2,1)}, bf16[1024,512]{1,0:T(8,128)(2,1)S(1)}, u32[]{:S(2)}, u32[]{:S(2)}) %collective-permute-start.26) | collective-permute-done | bytes 1048608 | tf_op jit(solution)/shard_map/ppermute | solution.py:43
  149.8 3.9 %collective-permute-start.22 = (bf16[512,512]{1,0:T(8,128)(2,1)}, bf16[512,512]{1,0:T(8,128)(2,1)}, u32[]{:S(2)}, u32[]{:S(2)}) collective-permute-start(bf16[512,512]{1,0:T(8,128)(2,1)} %collective-permute-done.20.refs_6_), channel_id=1, source_target_pairs={{0,8},{8,0},{16,24},{24,16},{32,40},{40,32},{48,56},{56,48},{64,72... | collective-permute-start | bytes 1572872 | tf_op jit(solution)/shard_map/ppermute | solution.py:43
  158.6 21.3 %shard_map.75.refs_1_ = bf16[256,1024]{1,0:T(8,128)(2,1)} custom-call(s32[2,8]{1,0:T(2,128)} %pad_add_fusion.bounds, bf16[256,512]{1,0:T(8,128)(2,1)} %get-tuple-element.35.perm, bf16[512,1024]{1,0:T(8,128)(2,1)} %bitcast.59, s32[4,1,512]{2,1,0:T(1,128)} %slice.203.offs, s32[4,1,512]{2,1,0:T(1,128)} %slice.206.starts, bf16[8192,128]{1,0:T(8,128)(2,1)} %k.3, ...), custom_call_target="tpu_custom_call" | custom-call | tf_op jit(solution)/shard_map/pallas_call | solution.py:289
  179.9 5.1 %shard_map.76 = bf16[512,1024]{1,0:T(8,128)(2,1)} custom-call(s32[2,8]{1,0:T(2,128)} %pad_add_fusion.bounds, bf16[256,512]{1,0:T(8,128)(2,1)} %get-tuple-element.36.perm, bf16[512,1024]{1,0:T(8,128)(2,1)} %bitcast.60, s32[4,1,512]{2,1,0:T(1,128)} %slice.196.offs, s32[4,1,512]{2,1,0:T(1,128)} %slice.199.starts, bf16[8192,128]{1,0:T(8,128)(2,1)} %k.3, ...), custom_call_target="tpu_custom_call" | custom-call | tf_op jit(solution)/shard_map/pallas_call | solution.py:289
  185.0 10.3 %all-to-all-start.2 = ((bf16[16,32,1024]{2,1,0:T(8,128)(2,1)}), bf16[16,32,1024]{2,1,0:T(8,128)(2,1)S(1)}, u32[]{:S(2)}, u32[]{:S(2)}) async-start(bf16[16,32,1024]{2,1,0:T(8,128)(2,1)} %bitcast.62), calls=%async_computation.2 | async-start | bytes 2097152 | tf_op jit(solution)/shard_map/all_to_all | solution.py:306
  199.1 22.3 %collective-permute-done.30.refs_16_ = bf16[512,512]{1,0:T(8,128)(2,1)} collective-permute-done((bf16[512,512]{1,0:T(8,128)(2,1)S(1)}, bf16[512,512]{1,0:T(8,128)(2,1)}, u32[]{:S(2)}, u32[]{:S(2)}) %collective-permute-start.30) | collective-permute-done | bytes 524320 | tf_op jit(solution)/shard_map/ppermute | solution.py:43
  224.9 11.6 %project.1 = (bf16[4,2,128,1024]{3,2,1,0:T(8,128)(2,1)}, bf16[4,128,1024]{2,1,0:T(8,128)(2,1)}, bf16[4,128,1024]{2,1,0:T(8,128)(2,1)}) custom-call(s32[5]{0:T(128)} %stack.42.place, bf16[256,1024]{1,0:T(8,128)(2,1)} %convolution_convert_fusion.1.rows, bf16[1024,512]{1,0:T(8,128)(2,1)} %refs_0_.2, bf16[1024,512]{1,0:T(8,128)(2,1)} %collective-permute-done.15.refs_1_, ...), custom_call_target="tpu_custom_call" | custom-call | tf_op jit(solution)/shard_map/project/pallas_call | solution.py:174
  239.2 3.1 %collective-permute-start.38 = (bf16[2,64,1024]{2,1,0:T(8,128)(2,1)S(1)}, bf16[2,64,1024]{2,1,0:T(8,128)(2,1)S(1)}, u32[]{:S(2)}, u32[]{:S(2)}) collective-permute-start(bf16[2,64,1024]{2,1,0:T(8,128)(2,1)S(1)} %get-tuple-element.33), channel_id=1, source_target_pairs={{0,3},{1,0},{2,1},{3,2},{4,7},{5,4},{6,5},{7,6},{8,11},{9,8},{10,9... | collective-permute-start | bytes 786440 | tf_op jit(solution)/shard_map/ppermute | solution.py:47
  243.9 4.3 %collective-permute-done.35 = bf16[2,64,1024]{2,1,0:T(8,128)(2,1)S(1)} collective-permute-done((bf16[2,64,1024]{2,1,0:T(8,128)(2,1)S(1)}, bf16[2,64,1024]{2,1,0:T(8,128)(2,1)S(1)}, u32[]{:S(2)}, u32[]{:S(2)}) %collective-permute-start.35) | collective-permute-done | bytes 262176 | tf_op jit(solution)/shard_map/ppermute | solution.py:47
  251.2 10.0 %collective-permute-done.41 = bf16[4,128,1024]{2,1,0:T(8,128)(2,1)S(1)} collective-permute-done((bf16[4,128,1024]{2,1,0:T(8,128)(2,1)}, bf16[4,128,1024]{2,1,0:T(8,128)(2,1)S(1)}, u32[]{:S(2)}, u32[]{:S(2)}) %collective-permute-start.41) | collective-permute-done | bytes 1048608 | tf_op jit(solution)/shard_map/ppermute | solution.py:47
  262.4 3.1 %collective-permute-start.42 = (bf16[1,64,1024]{2,1,0:T(8,128)(2,1)S(1)}, bf16[1,64,1024]{2,1,0:T(8,128)(2,1)S(1)}, u32[]{:S(2)}, u32[]{:S(2)}) collective-permute-start(bf16[1,64,1024]{2,1,0:T(8,128)(2,1)S(1)} %get-tuple-element.27), channel_id=1, source_target_pairs={{0,3},{1,0},{2,1},{3,2},{4,7},{5,4},{6,5},{7,6},{8,11},{9,8},{10,9... | collective-permute-start | bytes 393224 | tf_op jit(solution)/shard_map/ppermute | solution.py:47
  (175 shorter events, 82.2 us)
Async XLA Ops:
  0.0 26.5 %collective-permute-start.6 = (bf16[512,1024]{1,0:T(8,128)(2,1)}, bf16[512,1024]{1,0:T(8,128)(2,1)S(1)}, u32[]{:S(2)}, u32[]{:S(2)}) collective-permute-start(bf16[512,1024]{1,0:T(8,128)(2,1)} %refs_1_.1), channel_id=1, source_target_pairs={{0,32},{8,40},{16,48},{24,56},{32,64},{40,72},{48,80},{56,88},{64,... | collective-permute-start | bytes 3145736 | tf_op jit(solution)/shard_map/ppermute | solution.py:43
  7.2 27.8 %collective-permute-start.5 = (bf16[512,1024]{1,0:T(8,128)(2,1)}, bf16[512,1024]{1,0:T(8,128)(2,1)S(1)}, u32[]{:S(2)}, u32[]{:S(2)}) collective-permute-start(bf16[512,1024]{1,0:T(8,128)(2,1)} %refs_1_.1), channel_id=1, source_target_pairs={{0,8},{8,0},{16,24},{24,16},{32,40},{40,32},{48,56},{56,48},{64,72... | collective-permute-start | bytes 3145736 | tf_op jit(solution)/shard_map/ppermute | solution.py:43
  32.3 26.1 %collective-permute-start.7 = (bf16[512,1024]{1,0:T(8,128)(2,1)S(1)}, bf16[512,1024]{1,0:T(8,128)(2,1)}, u32[]{:S(2)}, u32[]{:S(2)}) collective-permute-start(bf16[512,1024]{1,0:T(8,128)(2,1)S(1)} %collective-permute-done.6.refs_7_.refs_3_), channel_id=1, source_target_pairs={{0,8},{8,0},{16,24},{24,16},{32,40},{40,32},{48,56},{56,48},{64,72... | collective-permute-start | bytes 3145736 | tf_op jit(solution)/shard_map/ppermute | solution.py:43
  34.9 25.0 %collective-permute-start.9 = (bf16[512,1024]{1,0:T(8,128)(2,1)S(1)}, bf16[512,1024]{1,0:T(8,128)(2,1)}, u32[]{:S(2)}, u32[]{:S(2)}) collective-permute-start(bf16[512,1024]{1,0:T(8,128)(2,1)S(1)} %collective-permute-done.8.refs_9_.refs_5_), channel_id=1, source_target_pairs={{0,8},{8,0},{16,24},{24,16},{32,40},{40,32},{48,56},{56,48},{64,72... | collective-permute-start | bytes 3145736 | tf_op jit(solution)/shard_map/ppermute | solution.py:43
  52.2 59.8 %collective-permute-start.24 = (bf16[1024,512]{1,0:T(8,128)(2,1)}, bf16[1024,512]{1,0:T(8,128)(2,1)}, u32[]{:S(2)}, u32[]{:S(2)}) collective-permute-start(bf16[1024,512]{1,0:T(8,128)(2,1)} %refs_0_.2), channel_id=1, source_target_pairs={{0,16},{8,24},{16,0},{24,8},{32,48},{40,56},{48,32},{56,40},{64,80... | collective-permute-start | bytes 3145736 | tf_op jit(solution)/shard_map/ppermute | solution.py:43
  55.0 50.7 %collective-permute-start.16 = (bf16[1024,512]{1,0:T(8,128)(2,1)}, bf16[1024,512]{1,0:T(8,128)(2,1)}, u32[]{:S(2)}, u32[]{:S(2)}) collective-permute-start(bf16[1024,512]{1,0:T(8,128)(2,1)} %refs_0_.2), channel_id=1, source_target_pairs={{0,32},{8,40},{16,48},{24,56},{32,64},{40,72},{48,80},{56,88},{64,... | collective-permute-start | bytes 3145736 | tf_op jit(solution)/shard_map/ppermute | solution.py:43
  55.6 52.5 %collective-permute-start.18 = (bf16[1024,512]{1,0:T(8,128)(2,1)}, bf16[1024,512]{1,0:T(8,128)(2,1)}, u32[]{:S(2)}, u32[]{:S(2)}) collective-permute-start(bf16[1024,512]{1,0:T(8,128)(2,1)} %refs_0_.2), channel_id=1, source_target_pairs={{0,96},{8,104},{16,112},{24,120},{32,0},{40,8},{48,16},{56,24},{64... | collective-permute-start | bytes 3145736 | tf_op jit(solution)/shard_map/ppermute | solution.py:43
  58.3 137.0 %collective-permute-start.15 = (bf16[1024,512]{1,0:T(8,128)(2,1)}, bf16[1024,512]{1,0:T(8,128)(2,1)}, u32[]{:S(2)}, u32[]{:S(2)}) collective-permute-start(bf16[1024,512]{1,0:T(8,128)(2,1)} %refs_0_.2), channel_id=1, source_target_pairs={{0,8},{8,0},{16,24},{24,16},{32,40},{40,32},{48,56},{56,48},{64,72... | collective-permute-start | bytes 3145736 | tf_op jit(solution)/shard_map/ppermute | solution.py:43
  66.4 52.3 %collective-permute-start.14 = (f32[256,1024]{1,0:T(8,128)}, f32[256,1024]{1,0:T(8,128)S(1)}, u32[]{:S(2)}, u32[]{:S(2)}) collective-permute-start(f32[256,1024]{1,0:T(8,128)} %shard_map.73), channel_id=1, source_target_pairs={{0,16},{8,24},{16,0},{24,8},{32,48},{40,56},{48,32},{56,40},{64,80... | collective-permute-start | bytes 3145736 | tf_op jit(solution)/shard_map/ppermute | solution.py:43
  67.7 36.6 %all-to-all-start = ((s32[16,1,32]{2,1,0:T(1,128)}), s32[16,1,32]{2,1,0:T(1,128)S(1)}, u32[]{:S(2)}, u32[]{:S(2)}) async-start(s32[16,1,32]{2,1,0:T(1,128)} %sub.40), calls=%async_computation | async-start | bytes 16384 | tf_op jit(solution)/shard_map/all_to_all | solution.py:306
  112.1 37.7 %collective-permute-start.26 = (bf16[1024,512]{1,0:T(8,128)(2,1)}, bf16[1024,512]{1,0:T(8,128)(2,1)S(1)}, u32[]{:S(2)}, u32[]{:S(2)}) collective-permute-start(bf16[1024,512]{1,0:T(8,128)(2,1)} %collective-permute-done.24.refs_10_), channel_id=1, source_target_pairs={{0,32},{8,40},{16,48},{24,56},{32,64},{40,72},{48,80},{56,88},{64,... | collective-permute-start | bytes 3145736 | tf_op jit(solution)/shard_map/ppermute | solution.py:43
  118.6 35.0 %collective-permute-start.28 = (bf16[1024,512]{1,0:T(8,128)(2,1)}, bf16[1024,512]{1,0:T(8,128)(2,1)S(1)}, u32[]{:S(2)}, u32[]{:S(2)}) collective-permute-start(bf16[1024,512]{1,0:T(8,128)(2,1)} %collective-permute-done.24.refs_10_), channel_id=1, source_target_pairs={{0,96},{8,104},{16,112},{24,120},{32,0},{40,8},{48,16},{56,24},{64... | collective-permute-start | bytes 3145736 | tf_op jit(solution)/shard_map/ppermute | solution.py:43
  124.8 32.8 %all-to-all-start.1 = ((bf16[16,32,1024]{2,1,0:T(8,128)(2,1)}), bf16[16,32,1024]{2,1,0:T(8,128)(2,1)S(1)}, u32[]{:S(2)}, u32[]{:S(2)}) async-start(bf16[16,32,1024]{2,1,0:T(8,128)(2,1)} %bitcast.11), calls=%async_computation.1 | async-start | bytes 2097152 | tf_op jit(solution)/shard_map/all_to_all | solution.py:306
  131.1 66.6 %collective-permute-start.25 = (bf16[1024,512]{1,0:T(8,128)(2,1)}, bf16[1024,512]{1,0:T(8,128)(2,1)}, u32[]{:S(2)}, u32[]{:S(2)}) collective-permute-start(bf16[1024,512]{1,0:T(8,128)(2,1)} %collective-permute-done.24.refs_10_), channel_id=1, source_target_pairs={{0,8},{8,0},{16,24},{24,16},{32,40},{40,32},{48,56},{56,48},{64,72... | collective-permute-start | bytes 3145736 | tf_op jit(solution)/shard_map/ppermute | solution.py:43
  131.2 66.5 %collective-permute-start.17 = (bf16[1024,512]{1,0:T(8,128)(2,1)}, bf16[1024,512]{1,0:T(8,128)(2,1)}, u32[]{:S(2)}, u32[]{:S(2)}) collective-permute-start(bf16[1024,512]{1,0:T(8,128)(2,1)} %collective-permute-done.16.refs_2_), channel_id=1, source_target_pairs={{0,8},{8,0},{16,24},{24,16},{32,40},{40,32},{48,56},{56,48},{64,72... | collective-permute-start | bytes 3145736 | tf_op jit(solution)/shard_map/ppermute | solution.py:43
  149.8 45.8 %collective-permute-start.22 = (bf16[512,512]{1,0:T(8,128)(2,1)}, bf16[512,512]{1,0:T(8,128)(2,1)}, u32[]{:S(2)}, u32[]{:S(2)}) collective-permute-start(bf16[512,512]{1,0:T(8,128)(2,1)} %collective-permute-done.20.refs_6_), channel_id=1, source_target_pairs={{0,8},{8,0},{16,24},{24,16},{32,40},{40,32},{48,56},{56,48},{64,72... | collective-permute-start | bytes 1572872 | tf_op jit(solution)/shard_map/ppermute | solution.py:43
  153.7 43.6 %collective-permute-start.23 = (bf16[512,512]{1,0:T(8,128)(2,1)}, bf16[512,512]{1,0:T(8,128)(2,1)}, u32[]{:S(2)}, u32[]{:S(2)}) collective-permute-start(bf16[512,512]{1,0:T(8,128)(2,1)} %collective-permute-done.21.refs_7_), channel_id=1, source_target_pairs={{0,8},{8,0},{16,24},{24,16},{32,40},{40,32},{48,56},{56,48},{64,72... | collective-permute-start | bytes 1572872 | tf_op jit(solution)/shard_map/ppermute | solution.py:43
  185.0 37.9 %all-to-all-start.2 = ((bf16[16,32,1024]{2,1,0:T(8,128)(2,1)}), bf16[16,32,1024]{2,1,0:T(8,128)(2,1)S(1)}, u32[]{:S(2)}, u32[]{:S(2)}) async-start(bf16[16,32,1024]{2,1,0:T(8,128)(2,1)} %bitcast.62), calls=%async_computation.2 | async-start | bytes 2097152 | tf_op jit(solution)/shard_map/all_to_all | solution.py:306
  195.4 28.8 %collective-permute-start.19 = (bf16[1024,512]{1,0:T(8,128)(2,1)}, bf16[1024,512]{1,0:T(8,128)(2,1)}, u32[]{:S(2)}, u32[]{:S(2)}) collective-permute-start(bf16[1024,512]{1,0:T(8,128)(2,1)} %collective-permute-done.18.refs_4_), channel_id=1, source_target_pairs={{0,8},{8,0},{16,24},{24,16},{32,40},{40,32},{48,56},{56,48},{64,72... | collective-permute-start | bytes 3145736 | tf_op jit(solution)/shard_map/ppermute | solution.py:43
  195.6 25.7 %collective-permute-start.30 = (bf16[512,512]{1,0:T(8,128)(2,1)S(1)}, bf16[512,512]{1,0:T(8,128)(2,1)}, u32[]{:S(2)}, u32[]{:S(2)}) collective-permute-start(bf16[512,512]{1,0:T(8,128)(2,1)S(1)} %slice.243), channel_id=1, source_target_pairs={{0,32},{8,40},{16,48},{24,56},{32,64},{40,72},{48,80},{56,88},{64,... | collective-permute-start | bytes 1572872 | tf_op jit(solution)/shard_map/ppermute | solution.py:43
  197.2 27.0 %collective-permute-start.27 = (bf16[1024,512]{1,0:T(8,128)(2,1)S(1)}, bf16[1024,512]{1,0:T(8,128)(2,1)}, u32[]{:S(2)}, u32[]{:S(2)}) collective-permute-start(bf16[1024,512]{1,0:T(8,128)(2,1)S(1)} %collective-permute-done.26.refs_12_), channel_id=1, source_target_pairs={{0,8},{8,0},{16,24},{24,16},{32,40},{40,32},{48,56},{56,48},{64,72... | collective-permute-start | bytes 3145736 | tf_op jit(solution)/shard_map/ppermute | solution.py:43
  197.6 26.6 %collective-permute-start.29 = (bf16[1024,512]{1,0:T(8,128)(2,1)S(1)}, bf16[1024,512]{1,0:T(8,128)(2,1)}, u32[]{:S(2)}, u32[]{:S(2)}) collective-permute-start(bf16[1024,512]{1,0:T(8,128)(2,1)S(1)} %collective-permute-done.28.refs_14_), channel_id=1, source_target_pairs={{0,8},{8,0},{16,24},{24,16},{32,40},{40,32},{48,56},{56,48},{64,72... | collective-permute-start | bytes 3145736 | tf_op jit(solution)/shard_map/ppermute | solution.py:43
  197.8 24.5 %collective-permute-start.31 = (bf16[512,512]{1,0:T(8,128)(2,1)S(1)}, bf16[512,512]{1,0:T(8,128)(2,1)}, u32[]{:S(2)}, u32[]{:S(2)}) collective-permute-start(bf16[512,512]{1,0:T(8,128)(2,1)S(1)} %slice.244), channel_id=1, source_target_pairs={{0,96},{8,104},{16,112},{24,120},{32,0},{40,8},{48,16},{56,24},{64... | collective-permute-start | bytes 1572872 | tf_op jit(solution)/shard_map/ppermute | solution.py:43
  236.5 24.6 %collective-permute-start.41 = (bf16[4,128,1024]{2,1,0:T(8,128)(2,1)}, bf16[4,128,1024]{2,1,0:T(8,128)(2,1)S(1)}, u32[]{:S(2)}, u32[]{:S(2)}) collective-permute-start(bf16[4,128,1024]{2,1,0:T(8,128)(2,1)} %get-tuple-element.20), channel_id=1, source_target_pairs={{0,4},{1,5},{2,6},{3,7},{4,0},{5,1},{6,2},{7,3},{8,12},{9,13},{10,... | collective-permute-start | bytes 3145736 | tf_op jit(solution)/shard_map/ppermute | solution.py:47
  (40 other events, 617.4 us)
